TPU v7x, 32 devices: a whole 2x2x4 slice. The times are simulated.
32 devices in a mesh: lev: 4 (over y, x), wave: 8 (over z, core).
Axes of the slice: x: 2, y: 2, z: 4, core: 2. Of those that a mesh axis runs over, the one named last changes fastest.
Arguments:
- vorticity: float32 [2, 32, 640, 640], P(None, 'lev', 'wave'), may hold values from -6 to 6
- wind_lam: float32 [32, 640, 1280], P('lev', 'wave'), may hold values from -6 to 6
- wind_mu: float32 [32, 640, 1280], P('lev', 'wave'), may hold values from -6 to 6
- modes: float32 [32, 32], replicated, may hold values from -0.5 to 1.5, as said below
- mode_rates: float32 [32], replicated, may hold values from 0.05 to 2
- wave_order: int32 [640], replicated, may hold values from 0 to 639, each once
- lat_order: int32 [640], replicated, may hold values from 0 to 639, each once
Outputs:
- advanced: float32 [2, 32, 640, 640], P(None, 'lev', 'wave')
- stream: float32 [2, 32, 640, 640], P(None, 'lev', 'wave')
Inputs may be any that keep to these rules, and one draw needn't show every extreme that they name: `wave_order`: A permutation: each wavenumber 0 to 639 is held by exactly one slot. `lat_order`: A permutation: each latitude 0 to 639 is held by exactly one slot. `modes`: A dense real matrix.
All inputs are finite; a program needn't handle non-finite values.
Results may differ from a plain program's by a relative error of at most 0.0003.
Values sent between devices are 32-bit elements; how exact they have to be, the bound alone decides.
A program may use at most 320 MiB of HBM per device.

v0:
```python
import functools
import math

import jax
import jax.numpy as jnp
from jax import lax
from jax.experimental import pallas as pl
from jax.experimental.pallas import tpu as pltpu
from jax.sharding import PartitionSpec as P

M = 640
LAT = 640
GRID_LONGITUDES = 1280


HIGH_ACCURACY = lax.Precision.HIGH
TIME_STEP = 0.4


def latitudes(lat_order):
    angles = math.pi * (lat_order.astype(jnp.float32) + 0.75) / (LAT + 0.5)
    sines = jnp.sin(angles)
    return (jnp.cos(angles), sines, math.pi / (LAT + 0.5) * sines)


GROUP = 8
PARTS = 2
LANES = 128
VMEM = 60 * 1024 * 1024


def table_kernel(ahead_ref, behind_ref, start_ref, cos_ref, out_ref):
    lats = out_ref.shape[2]
    spans = [(k, min(LANES, lats - k)) for k in range(0, lats, LANES)]
    mus = [jnp.broadcast_to(cos_ref[0:1, k : k + n], (GROUP, n)) for k, n in spans]

    def block(index, carry):
        first = pl.multiple_of(index * 8, 8)
        ahead = [ahead_ref[first + t] for t in range(8)]
        behind = [behind_ref[first + t] for t in range(8)]
        following_carry = []
        for (k, n), mu, (previous, current, log_scale) in zip(spans, mus, carry):
            scale = jnp.exp(log_scale)
            rows = []
            for t in range(8):
                rows.append(current * scale)
                following = ahead[t][:, :n] * (mu * current - behind[t][:, :n] * previous)
                previous, current = current, following
            magnitude = jnp.abs(previous) + jnp.abs(current)
            following_carry.append(
                (previous / magnitude, current / magnitude, log_scale + jnp.log(magnitude))
            )
            out_ref[:, pl.ds(first, 8), k : k + n] = jnp.swapaxes(jnp.stack(rows), 0, 1)
        return tuple(following_carry)

    initial = tuple(
        (
            jnp.zeros((GROUP, n), jnp.float32),
            jnp.ones((GROUP, n), jnp.float32),
            start_ref[:, k : k + n],
        )
        for k, n in spans
    )
    lax.fori_loop(0, out_ref.shape[1] // 8, block, initial)


def legendre(waves, cosines, sines, degrees):
    wavenum = waves.astype(jnp.float32)[:, None]
    counter = jnp.arange(1, M, dtype=jnp.int32).astype(jnp.float32)
    halves = 0.5 * jnp.log((2.0 * counter + 1.0) / (2.0 * counter))
    start_log = jnp.sum(jnp.where(counter[None, :] <= wavenum, halves[None, :], 0.0), axis=1)
    log_start = -0.5 * math.log(2.0) + start_log[:, None] + wavenum * jnp.log(sines)[None, :]
    degree = wavenum.T + jnp.arange(degrees, dtype=jnp.int32).astype(jnp.float32)[:, None] + 1.0
    square = wavenum.T * wavenum.T
    ahead = jnp.sqrt((4.0 * degree * degree - 1.0) / (degree * degree - square))
    lower = degree - 1.0
    behind = jnp.sqrt((lower * lower - square) / (4.0 * lower * lower - 1.0))
    slots, lats = waves.shape[0], cosines.shape[0]
    wide = (degrees, slots, LANES)
    coefficient = pl.BlockSpec((degrees, GROUP, LANES), lambda g: (0, g, 0))
    return pl.pallas_call(
        table_kernel,
        grid=(slots // GROUP,),
        in_specs=[
            coefficient,
            coefficient,
            pl.BlockSpec((GROUP, lats), lambda g: (g, 0)),
            pl.BlockSpec((1, lats), lambda g: (0, 0)),
        ],
        out_specs=pl.BlockSpec((GROUP, degrees, lats), lambda g: (g, 0, 0)),
        out_shape=jax.ShapeDtypeStruct((slots, degrees, lats), jnp.float32),
        compiler_params=pltpu.CompilerParams(vmem_limit_bytes=VMEM),
        name="table",
    )(
        jnp.broadcast_to(ahead[:, :, None], wide),
        jnp.broadcast_to(behind[:, :, None], wide),
        log_start,
        cosines[None, :],
    )


def halves_of(value):
    high = value.astype(jnp.bfloat16)
    return high, (value - high.astype(jnp.float32)).astype(jnp.bfloat16)


def three_products(fields, table, contract):
    rows = fields.shape[0]
    field_high, field_low = halves_of(fields)
    table_high, table_low = halves_of(table)
    dims = (((1,), (contract,)), ((), ()))
    both = lax.dot_general(
        jnp.concatenate([field_high, field_low], axis=0),
        table_high,
        dims,
        preferred_element_type=jnp.float32,
    )
    small = lax.dot_general(field_high, table_low, dims, preferred_element_type=jnp.float32)
    return both[:rows] + (both[rows:] + small)


def transform_kernel(waves_ref, fields_ref, table_ref, after_ref, out_ref, turned, result, *, forward):
    degrees = table_ref.shape[1]
    turned[...] = jnp.swapaxes(fields_ref[...], 0, 1)
    group = pl.program_id(0)

    def one_slot(i, carry):
        alive = degrees - waves_ref[group * GROUP + i]
        for first in range(0, degrees, 256):
            last = min(first + 256, degrees)

            @pl.when(alive > first)
            def _():
                table = table_ref[i, first:last, :]
                if forward:
                    result[i, :, first:last] = three_products(turned[i], table, 1)
                elif first == 0:
                    result[i] = three_products(turned[i, :, first:last], table, 0)
                else:
                    result[i] += three_products(turned[i, :, first:last], table, 0)

            if forward:

                @pl.when(alive <= first)
                def _():
                    result[i, :, first:last] = jnp.zeros(
                        (result.shape[1], last - first), jnp.float32
                    )

        return carry

    lax.fori_loop(0, GROUP, one_slot, 0)
    out_ref[...] = jnp.swapaxes(result[...], 0, 1)


def transform(waves, fields, table, after, forward):
    rows, slots, width = fields.shape
    degrees, lats = table.shape[1:]
    out_width = degrees if forward else lats
    return pl.pallas_call(
        functools.partial(transform_kernel, forward=forward),
        grid_spec=pltpu.PrefetchScalarGridSpec(
            num_scalar_prefetch=1,
            grid=(slots // GROUP,),
            in_specs=[
                pl.BlockSpec((rows, GROUP, width), lambda g, w: (0, g, 0)),
                pl.BlockSpec((GROUP, degrees, lats), lambda g, w: (g, 0, 0)),
                pl.BlockSpec(memory_space=pl.ANY),
            ],
            out_specs=pl.BlockSpec((rows, GROUP, out_width), lambda g, w: (0, g, 0)),
            scratch_shapes=[
                pltpu.VMEM((GROUP, rows, width), jnp.float32),
                pltpu.VMEM((GROUP, rows, out_width), jnp.float32),
            ],
        ),
        out_shape=jax.ShapeDtypeStruct((rows, slots, out_width), jnp.float32),
        compiler_params=pltpu.CompilerParams(vmem_limit_bytes=VMEM),
        name="analysis" if forward else "synthesis",
    )(waves, fields, table, after)


def padded(array, axis, size):
    widths = [(0, 0)] * array.ndim
    widths[axis] = (0, size - array.shape[axis])
    return jnp.pad(array, widths) if size > array.shape[axis] else array


def coupling(waves):
    wavenum = waves.astype(jnp.float32)[:, None]
    degree = wavenum + jnp.arange(M, dtype=jnp.int32).astype(jnp.float32)[None, :]
    live_mask = (degree < M - 0.5).astype(jnp.float32)
    square = wavenum * wavenum
    eps_here = jnp.sqrt((degree * degree - square) / (4.0 * degree * degree - 1.0))
    degree_next = degree + 1.0
    eps_ahead = jnp.sqrt(
        (degree_next * degree_next - square) / (4.0 * degree_next * degree_next - 1.0)
    )
    kappa = degree * (degree + 1.0) / (M * (M + 1.0))
    return (
        -(degree - 1.0) * eps_here * live_mask,
        (degree + 2.0) * eps_ahead * live_mask,
        live_mask,
        kappa,
    )


def fourier(waves):
    phase = waves[:, None] * jnp.arange(GRID_LONGITUDES, dtype=jnp.int32)[None, :] % GRID_LONGITUDES
    angles = 2.0 * math.pi / GRID_LONGITUDES * phase.astype(jnp.float32)
    return jnp.concatenate([jnp.cos(angles), jnp.sin(angles)], axis=0)


def lowered(spectra):
    return jnp.concatenate([jnp.zeros_like(spectra[..., :1]), spectra[..., :-1]], axis=-1)


def raised(spectra):
    return jnp.concatenate([spectra[..., 1:], jnp.zeros_like(spectra[..., :1])], axis=-1)


def on_device(vorticity, wind_lam, wind_mu, modes, mode_rates, wave_order, lat_order):
    slots = vorticity.shape[2]
    wave_pos = lax.axis_index("wave")
    lev_pos = lax.axis_index("lev")
    waves = lax.dynamic_slice_in_dim(wave_order, wave_pos * slots, slots)
    cosines, sines, weights = latitudes(lat_order)
    full = -(-slots // GROUP) * GROUP
    full_waves = padded(waves, 0, full)
    legendre_table = legendre(full_waves, cosines, sines, M)
    lower, upper, live_mask, kappa = coupling(waves)
    trigonometric_table = fourier(wave_order)
    double = jnp.where(wave_order == 0, 1.0, 2.0).astype(jnp.float32)
    scaled = double * wave_order.astype(jnp.float32)

    def synthesis(spectra, after):
        meridional = lower * lowered(spectra) + upper * raised(spectra)
        both = jnp.stack([spectra, meridional])
        rows = both.shape[0] * both.shape[1] * both.shape[2]
        flat = padded(both.reshape(rows, slots, M), 1, full)
        at_lat = transform(full_waves, flat, legendre_table, after, False)[:, :slots]
        return at_lat.reshape(both.shape[:4] + (LAT,))

    def to_latitudes(at_lat):
        return lax.all_to_all(at_lat, "wave", split_axis=4, concat_axis=3, tiled=True)

    def products(at_lat, part_lam, part_mu):
        zonal = jnp.concatenate(
            [-(scaled[:, None] * at_lat[0, 1]), -(scaled[:, None] * at_lat[0, 0])], axis=1
        )
        merid = jnp.concatenate(
            [double[:, None] * at_lat[1, 0], -(double[:, None] * at_lat[1, 1])], axis=1
        )
        grid = jnp.einsum(
            "flsr,sk->flrk", jnp.stack([zonal, merid]), trigonometric_table, precision=HIGH_ACCURACY
        )
        source_term = -(part_lam * grid[0] + part_mu * grid[1])
        spectral_latitude_fields = (
            jnp.einsum("nqy,zy->nzq", source_term, trigonometric_table, precision=HIGH_ACCURACY)
            / GRID_LONGITUDES
        )
        return jnp.stack([spectral_latitude_fields[:, :M], -spectral_latitude_fields[:, M:]])

    def to_waves(returned):
        return lax.all_to_all(returned, "wave", split_axis=2, concat_axis=3, tiled=True)

    def analysis(returned, after):
        returned = returned * weights
        flat = padded(returned.reshape(-1, slots, LAT), 1, full)
        result = transform(full_waves, flat, legendre_table, after, True)[:, :slots]
        return result.reshape(returned.shape[:3] + (M,)) * live_mask

    def token(array):
        corner = array[(0,) * (array.ndim - 2)]
        return lax.slice(corner, (0, 0), (min(8, corner.shape[0]), min(LANES, corner.shape[1])))

    def ordered(array, earlier):
        return array + 0.0 * token(earlier)[0, 0]

    levels = vorticity.shape[1]
    step = levels // PARTS if levels % PARTS == 0 else levels
    parts = [slice(first, first + step) for first in range(0, levels, step)]
    lev_count = modes.shape[0] // levels
    grouped = modes.reshape(lev_count, levels, modes.shape[1])
    rows_of = [grouped[:, part].reshape(lev_count * step, -1) for part in parts]
    winds = [(wind_lam[part], wind_mu[part]) for part in parts]
    starts = [vorticity[:, part] * live_mask for part in parts]
    count = len(parts)
    last = cosines[None, :]

    at_lats = []
    for start in starts:
        at_lats.append(synthesis(start, last))
        last = token(at_lats[-1])
    landed = [token(cosines[None, None, :])]

    def in_turn(exchange, array):
        moved = exchange(ordered(array, landed[0]))
        landed[0] = token(moved)
        return moved

    at_lats = [in_turn(to_latitudes, at_lat) for at_lat in at_lats]
    rates = []
    for stage in range(2):
        returned = []
        for at_lat, wind in zip(at_lats, winds):
            returned.append(products(ordered(at_lat, last), *wind))
            last = token(returned[-1])
        returned = [in_turn(to_waves, piece) for piece in returned]
        at_lats = []
        for index in range(count):
            rate = analysis(returned[index], last)
            last = token(rate)
            rates.append(rate)
            if stage == 0:
                middle = starts[index] + TIME_STEP / M * rate
                at_lats.append(synthesis(middle, last))
                last = token(at_lats[-1])
        at_lats = [in_turn(to_latitudes, at_lat) for at_lat in at_lats]
    advanced_parts = [
        starts[index] + 0.5 * TIME_STEP / M * (rates[index] + rates[count + index])
        for index in range(count)
    ]
    def to_blocks(array):
        return lax.all_to_all(array, "lev", split_axis=3, concat_axis=1, tiled=True)

    projected = 0.0
    for advanced, rows in zip(advanced_parts, rows_of):
        gathered = in_turn(to_blocks, advanced)
        projected = projected + jnp.einsum(
            "lk,clsj->cksj", rows, gathered, precision=HIGH_ACCURACY
        )
    block_width = projected.shape[3]
    diffusion_block = lax.dynamic_slice_in_dim(kappa, lev_pos * block_width, block_width, 1)
    projected = projected / (diffusion_block[None, None] + mode_rates[None, :, None, None])
    streams = []
    for rows in rows_of:
        restored = jnp.einsum("lk,cksj->clsj", rows, projected, precision=HIGH_ACCURACY)
        streams.append(lax.all_to_all(restored, "lev", split_axis=1, concat_axis=3, tiled=True))
    advanced = jnp.concatenate(advanced_parts, axis=1)
    stream = jnp.concatenate(streams, axis=1) * live_mask
    return (advanced, stream)


def solution(mesh):
    placed = (
        P(None, "lev", "wave", None),
        P("lev", "wave", None),
        P("lev", "wave", None),
        P(),
        P(),
        P(),
        P(),
    )
    return jax.shard_map(
        on_device,
        mesh=mesh,
        in_specs=placed,
        out_specs=(P(None, "lev", "wave", None), P(None, "lev", "wave", None)),
        check_vma=False,
    )
```

profile of v0, /device:TPU:0, one launch (start us, length us, event | category | flops | bytes accessed | tf_op | source)
XLA Modules:
  0.0 1389.5 jit_solution(3308919216447383405)
XLA Ops:
  13.3 9.2 broadcast_in_dim.26.ahead_ref
  22.5 9.2 broadcast_in_dim.27.behind_ref
  31.7 72.6 %table.1.table_ref = f32[80,640,640]{2,1,0:T(8,128)} custom-call(f32[640,80,128]{2,1,0:T(8,128)} %broadcast_in_dim.26.ahead_ref, f32[640,80,128]{2,1,0:T(8,128)} %broadcast_in_dim.27.behind_ref, f32[80,640]{1,0:T(8,128)} %get-tuple-element.78.start_ref, f32[1,640]{1,0:T(1,128)} %copy-done.39), custom_call_target="tpu_custom_call" | custom-call | tf_op jit(solution)/shard_map/table/pallas_call | solution.py:81
  104.3 47.2 %synthesis.4 = f32[16,80,640]{2,1,0:T(8,128)} custom-call(s32[80]{0:T(128)} %copy-done.36, f32[16,80,640]{2,1,0:T(8,128)} %bitcast.445, f32[80,640,640]{2,1,0:T(8,128)} %table.1.table_ref, f32[1,640]{1,0:T(1,128)} %copy-done.39), custom_call_target="tpu_custom_call" | custom-call | tf_op jit(solution)/shard_map/synthesis/pallas_call | solution.py:160
  152.1 3.9 broadcast_add_fusion.7
  156.0 6.5 copy.172
  162.5 6.4 all-to-all-start
  172.4 47.2 %synthesis.5 = f32[16,80,640]{2,1,0:T(8,128)} custom-call(s32[80]{0:T(128)} %copy-done.36, f32[16,80,640]{2,1,0:T(8,128)} %bitcast.444, f32[80,640,640]{2,1,0:T(8,128)} %table.1.table_ref, f32[8,128]{1,0:T(8,128)} %slice.418.after_ref), custom_call_target="tpu_custom_call" | custom-call | tf_op jit(solution)/shard_map/synthesis/pallas_call | solution.py:160
  219.5 65.9 %all-to-all-done = f32[2,2,4,80,640]{3,2,1,0,4:T(4,128)} async-done(((f32[2,2,4,80,640]{3,2,1,0,4:T(4,128)}), f32[2,2,4,80,640]{3,2,1,0,4:T(4,128)}, u32[]{:S(2)}, u32[]{:S(2)}) %all-to-all-start) | async-done | bytes 3276832 | tf_op jit(solution)/shard_map/all_to_all | solution.py:244
  285.5 6.9 copy.173
  296.2 6.4 copy.177
  302.6 5.0 all-to-all-start.1
  308.9 13.7 fusion.45
  322.6 5.3 broadcast_add_fusion.3
  328.8 8.8 fusion.6
  337.6 5.7 fusion.56
  345.1 78.8 %all-to-all-done.1 = f32[2,2,4,80,640]{3,2,1,0,4:T(4,128)} async-done(((f32[2,2,4,80,640]{3,2,1,0,4:T(4,128)}), f32[2,2,4,80,640]{3,2,1,0,4:T(4,128)}, u32[]{:S(2)}, u32[]{:S(2)}) %all-to-all-start.1) | async-done | bytes 3276832 | tf_op jit(solution)/shard_map/all_to_all | solution.py:244
  423.9 6.8 copy.178
  437.7 4.6 all-to-all-start.2
  449.8 8.8 fusion.4
  458.7 6.0 fusion.53
  466.3 36.1 %all-to-all-done.2 = f32[2,4,640,80]{3,1,0,2:T(4,128)} async-done(((f32[2,4,640,80]{3,1,0,2:T(4,128)}), f32[2,4,640,80]{3,1,0,2:T(4,128)}, u32[]{:S(2)}, u32[]{:S(2)}) %all-to-all-start.2) | async-done | bytes 1638432 | tf_op jit(solution)/shard_map/all_to_all | solution.py:264
  514.5 4.6 all-to-all-start.3
  522.1 57.3 %all-to-all-done.3 = f32[2,4,640,80]{3,1,0,2:T(4,128)} async-done(((f32[2,4,640,80]{3,1,0,2:T(4,128)}), f32[2,4,640,80]{3,1,0,2:T(4,128)}, u32[]{:S(2)}, u32[]{:S(2)}) %all-to-all-start.3) | async-done | bytes 1638432 | tf_op jit(solution)/shard_map/all_to_all | solution.py:264
  586.1 3.9 broadcast_multiply_fusion.3
  589.9 51.9 %analysis.4 = f32[8,80,640]{2,1,0:T(8,128)} custom-call(s32[80]{0:T(128)} %copy-done.36, f32[8,80,640]{2,1,0:T(8,128)} %get-tuple-element.69.fields_ref, f32[80,640,640]{2,1,0:T(8,128)} %table.1.table_ref, f32[8,80]{1,0:T(8,128)} %slice_bitcast_fusion.44.after_ref), custom_call_target="tpu_custom_call" | custom-call | tf_op jit(solution)/shard_map/analysis/pallas_call | solution.py:160
  649.9 47.2 %synthesis.6 = f32[16,80,640]{2,1,0:T(8,128)} custom-call(s32[80]{0:T(128)} %copy-done.36, f32[16,80,640]{2,1,0:T(8,128)} %bitcast.442, f32[80,640,640]{2,1,0:T(8,128)} %table.1.table_ref, f32[8,128]{1,0:T(8,128)} %slice.443.after_ref), custom_call_target="tpu_custom_call" | custom-call | tf_op jit(solution)/shard_map/synthesis/pallas_call | solution.py:160
  699.3 4.4 copy.188
  703.7 4.6 all-to-all-start.4
  709.9 51.9 %analysis.5 = f32[8,80,640]{2,1,0:T(8,128)} custom-call(s32[80]{0:T(128)} %copy-done.36, f32[8,80,640]{2,1,0:T(8,128)} %get-tuple-element.70.fields_ref, f32[80,640,640]{2,1,0:T(8,128)} %table.1.table_ref, f32[8,128]{1,0:T(8,128)} %slice.450.after_ref), custom_call_target="tpu_custom_call" | custom-call | tf_op jit(solution)/shard_map/analysis/pallas_call | solution.py:160
  767.6 47.2 %synthesis.7 = f32[16,80,640]{2,1,0:T(8,128)} custom-call(s32[80]{0:T(128)} %copy-done.36, f32[16,80,640]{2,1,0:T(8,128)} %bitcast.443, f32[80,640,640]{2,1,0:T(8,128)} %table.1.table_ref, f32[8,128]{1,0:T(8,128)} %slice.454.after_ref), custom_call_target="tpu_custom_call" | custom-call | tf_op jit(solution)/shard_map/synthesis/pallas_call | solution.py:160
  814.8 10.0 all-to-all-done.4
  824.8 6.9 copy.189
  835.6 6.5 copy.193
  842.0 5.1 all-to-all-start.5
  854.4 8.8 fusion.2
  863.2 5.7 fusion.50
  870.6 92.5 %all-to-all-done.5 = f32[2,2,4,80,640]{3,2,1,0,4:T(4,128)} async-done(((f32[2,2,4,80,640]{3,2,1,0,4:T(4,128)}), f32[2,2,4,80,640]{3,2,1,0,4:T(4,128)}, u32[]{:S(2)}, u32[]{:S(2)}) %all-to-all-start.5) | async-done | bytes 3276832 | tf_op jit(solution)/shard_map/all_to_all | solution.py:244
  963.1 6.8 copy.194
  976.9 4.4 all-to-all-start.6
  988.9 8.8 fusion
  997.7 6.0 fusion.47
  1005.3 36.4 %all-to-all-done.6 = f32[2,4,640,80]{3,1,0,2:T(4,128)} async-done(((f32[2,4,640,80]{3,1,0,2:T(4,128)}), f32[2,4,640,80]{3,1,0,2:T(4,128)}, u32[]{:S(2)}, u32[]{:S(2)}) %all-to-all-start.6) | async-done | bytes 1638432 | tf_op jit(solution)/shard_map/all_to_all | solution.py:264
  1053.8 4.4 all-to-all-start.7
  1061.2 57.3 %all-to-all-done.7 = f32[2,4,640,80]{3,1,0,2:T(4,128)} async-done(((f32[2,4,640,80]{3,1,0,2:T(4,128)}), f32[2,4,640,80]{3,1,0,2:T(4,128)}, u32[]{:S(2)}, u32[]{:S(2)}) %all-to-all-start.7) | async-done | bytes 1638432 | tf_op jit(solution)/shard_map/all_to_all | solution.py:264
  1127.3 3.8 broadcast_multiply_fusion
  1131.1 51.9 %analysis.6 = f32[8,80,640]{2,1,0:T(8,128)} custom-call(s32[80]{0:T(128)} %copy-done.36, f32[8,80,640]{2,1,0:T(8,128)} %get-tuple-element.68.fields_ref, f32[80,640,640]{2,1,0:T(8,128)} %table.1.table_ref, f32[8,80]{1,0:T(8,128)} %slice_bitcast_fusion.40.after_ref), custom_call_target="tpu_custom_call" | custom-call | tf_op jit(solution)/shard_map/analysis/pallas_call | solution.py:160
  1183.1 4.4 broadcast_add_fusion.10
  1187.5 3.8 copy.204
  1191.3 3.9 all-to-all-start.8
  1196.7 51.8 %analysis.7 = f32[8,80,640]{2,1,0:T(8,128)} custom-call(s32[80]{0:T(128)} %copy-done.36, f32[8,80,640]{2,1,0:T(8,128)} %get-tuple-element.67.fields_ref, f32[80,640,640]{2,1,0:T(8,128)} %table.1.table_ref, f32[8,128]{1,0:T(8,128)} %slice.480.after_ref), custom_call_target="tpu_custom_call" | custom-call | tf_op jit(solution)/shard_map/analysis/pallas_call | solution.py:160
  1250.0 4.7 copy.208
  1256.8 3.9 broadcast_add_fusion.9
  1264.5 4.7 all-to-all-start.9
  1275.8 19.2 %all-to-all-done.9 = f32[2,4,80,640]{2,1,0,3:T(4,128)} async-done(((f32[2,4,80,640]{2,1,0,3:T(4,128)}), f32[2,4,80,640]{2,1,0,3:T(4,128)}, u32[]{:S(2)}, u32[]{:S(2)}) %all-to-all-start.9) | async-done | bytes 1638432 | tf_op jit(solution)/shard_map/all_to_all | solution.py:324
  1295.0 4.0 copy.211
  1310.9 3.9 all-to-all-start.10
  1314.8 3.9 convolution_bitcast_fusion
  1321.8 23.0 %all-to-all-done.10 = f32[2,16,80,160]{3,2,0,1:T(8,128)S(1)} async-done(((f32[2,16,80,160]{3,2,0,1:T(8,128)}), f32[2,16,80,160]{3,2,0,1:T(8,128)S(1)}, u32[]{:S(2)}, u32[]{:S(2)}) %all-to-all-start.10) | async-done | bytes 1638432 | tf_op jit(solution)/shard_map/all_to_all | solution.py:338
  1344.8 4.6 all-to-all-start.11
  1349.3 3.8 pad_maximum_fusion.5
  1356.4 3.9 all_to_all.208
  1360.3 19.1 %all-to-all-done.11 = f32[2,16,80,160]{3,2,0,1:T(8,128)} async-done(((f32[2,16,80,160]{3,2,0,1:T(8,128)}), f32[2,16,80,160]{3,2,0,1:T(8,128)}, u32[]{:S(2)}, u32[]{:S(2)}) %all-to-all-start.11) | async-done | bytes 1638432 | tf_op jit(solution)/shard_map/all_to_all | solution.py:338
  1385.4 3.9 maximum_multiply_fusion
  (225 shorter events, 162.5 us)
Async XLA Ops:
  1.4 6.5 copy-start.36
  1.5 6.4 copy-start.17
  5.2 2.8 copy-start.39
  7.9 3.2 copy-start.10
  7.9 162.5 %copy-start.7 = (f32[2,4,80,640]{3,2,1,0:T(8,128)}, f32[2,4,80,640]{3,2,1,0:T(8,128)S(1)}, u32[]{:S(2)}) copy-start(f32[2,4,80,640]{3,2,1,0:T(8,128)S(1)} %get-tuple-element.38) | copy-start | bytes 4915204
  10.2 1.0 copy-start.22
  10.2 1.0 copy-start.25
  11.1 2.1 copy-start.30
  13.3 9.2 copy-start.31
  162.5 123.0 %all-to-all-start = ((f32[2,2,4,80,640]{3,2,1,0,4:T(4,128)}), f32[2,2,4,80,640]{3,2,1,0,4:T(4,128)}, u32[]{:S(2)}, u32[]{:S(2)}) async-start(f32[2,2,4,80,640]{3,2,1,0,4:T(4,128)} %copy.172), calls=%async_computation | async-start | bytes 10485760 | tf_op jit(solution)/shard_map/all_to_all | solution.py:244
  285.5 8.8 copy-start.15
  302.6 6.2 copy-start.40
  302.6 121.2 %all-to-all-start.1 = ((f32[2,2,4,80,640]{3,2,1,0,4:T(4,128)}), f32[2,2,4,80,640]{3,2,1,0,4:T(4,128)}, u32[]{:S(2)}, u32[]{:S(2)}) async-start(f32[2,2,4,80,640]{3,2,1,0,4:T(4,128)} %copy.177), calls=%async_computation.1 | async-start | bytes 10485760 | tf_op jit(solution)/shard_map/all_to_all | solution.py:244
  308.9 138.3 %copy-start.32 = (f32[640]{0:T(1024)}, f32[640]{0:T(1024)S(1)}, u32[]{:S(2)}) copy-start(f32[640]{0:T(1024)S(1)} %get-tuple-element.76) | copy-start | bytes 7684
  308.9 138.3 %copy-start.34 = (f32[640]{0:T(1024)}, f32[640]{0:T(1024)S(1)}, u32[]{:S(2)}) copy-start(f32[640]{0:T(1024)S(1)} %get-tuple-element.77) | copy-start | bytes 7684
  322.6 15.0 %copy-start.3 = (f32[640,1280]{1,0:T(8,128)}, f32[640,1280]{1,0:T(8,128)S(1)}, u32[]{:S(2)}) copy-start(f32[640,1280]{1,0:T(8,128)S(1)} %get-tuple-element.75) | copy-start | bytes 9830404
  322.6 136.0 %copy-start.1 = (f32[640,1280]{1,0:T(8,128)}, f32[640,1280]{1,0:T(8,128)S(1)}, u32[]{:S(2)}) copy-start(f32[640,1280]{1,0:T(8,128)S(1)} %get-tuple-element.74) | copy-start | bytes 9830404
  328.8 8.8 copy-start.43
  328.8 8.8 copy-start.47
  437.7 64.7 %all-to-all-start.2 = ((f32[2,4,640,80]{3,1,0,2:T(4,128)}), f32[2,4,640,80]{3,1,0,2:T(4,128)}, u32[]{:S(2)}, u32[]{:S(2)}) async-start(f32[2,4,640,80]{3,1,0,2:T(4,128)} %copy.180), calls=%async_computation.2 | async-start | bytes 5242880 | tf_op jit(solution)/shard_map/all_to_all | solution.py:264
  447.9 1.9 copy-start.4
  449.8 8.8 copy-start.44
  449.8 8.8 copy-start.48
  514.5 64.9 %all-to-all-start.3 = ((f32[2,4,640,80]{3,1,0,2:T(4,128)}), f32[2,4,640,80]{3,1,0,2:T(4,128)}, u32[]{:S(2)}, u32[]{:S(2)}) async-start(f32[2,4,640,80]{3,1,0,2:T(4,128)} %copy.186), calls=%async_computation.3 | async-start | bytes 5242880 | tf_op jit(solution)/shard_map/all_to_all | solution.py:264
  584.4 1.7 copy-start.37
  589.9 52.0 %copy-start.11 = (f32[2,4,80,640]{3,2,1,0:T(8,128)S(1)}, f32[2,4,80,640]{3,2,1,0:T(8,128)}, u32[]{:S(2)}) copy-start(f32[2,4,80,640]{3,2,1,0:T(8,128)} %copy-done.10) | copy-start | bytes 4915204
  589.9 52.0 %copy-start.18 = (f32[80,640]{1,0:T(8,128)S(1)}, f32[80,640]{1,0:T(8,128)}, u32[]{:S(2)}) copy-start(f32[80,640]{1,0:T(8,128)} %copy-done.17) | copy-start | bytes 614404
  643.5 1.2 copy-start.21
  643.6 3.9 copy-start.23
  643.6 3.9 copy-start.26
  703.7 121.1 %all-to-all-start.4 = ((f32[2,2,4,80,640]{3,2,1,0,4:T(4,128)}), f32[2,2,4,80,640]{3,2,1,0,4:T(4,128)}, u32[]{:S(2)}, u32[]{:S(2)}) async-start(f32[2,2,4,80,640]{3,2,1,0,4:T(4,128)} %copy.188), calls=%async_computation.4 | async-start | bytes 10485760 | tf_op jit(solution)/shard_map/all_to_all | solution.py:244
  709.9 51.9 %copy-start.8 = (f32[2,4,80,640]{3,2,1,0:T(8,128)S(1)}, f32[2,4,80,640]{3,2,1,0:T(8,128)}, u32[]{:S(2)}) copy-start(f32[2,4,80,640]{3,2,1,0:T(8,128)} %copy-done.7) | copy-start | bytes 4915204
  763.5 1.2 copy-start.20
  764.2 0.9 copy-start.24
  764.2 1.0 copy-start.27
  824.8 8.8 copy-start.16
  842.0 121.1 %all-to-all-start.5 = ((f32[2,2,4,80,640]{3,2,1,0,4:T(4,128)}), f32[2,2,4,80,640]{3,2,1,0,4:T(4,128)}, u32[]{:S(2)}, u32[]{:S(2)}) async-start(f32[2,2,4,80,640]{3,2,1,0,4:T(4,128)} %copy.193), calls=%async_computation.5 | async-start | bytes 10485760 | tf_op jit(solution)/shard_map/all_to_all | solution.py:244
  848.3 3.0 copy-start.33
  848.3 3.0 copy-start.35
  851.3 1.9 copy-start.5
  852.0 2.4 copy-start.2
  854.4 8.8 copy-start.45
  854.4 8.8 copy-start.49
  976.9 64.7 %all-to-all-start.6 = ((f32[2,4,640,80]{3,1,0,2:T(4,128)}), f32[2,4,640,80]{3,1,0,2:T(4,128)}, u32[]{:S(2)}, u32[]{:S(2)}) async-start(f32[2,4,640,80]{3,1,0,2:T(4,128)} %copy.196), calls=%async_computation.6 | async-start | bytes 5242880 | tf_op jit(solution)/shard_map/all_to_all | solution.py:264
  986.9 1.9 copy-start.6
  988.9 8.8 copy-start.46
  988.9 8.8 copy-start.50
  1053.8 64.7 %all-to-all-start.7 = ((f32[2,4,640,80]{3,1,0,2:T(4,128)}), f32[2,4,640,80]{3,1,0,2:T(4,128)}, u32[]{:S(2)}, u32[]{:S(2)}) async-start(f32[2,4,640,80]{3,1,0,2:T(4,128)} %copy.202), calls=%async_computation.7 | async-start | bytes 5242880 | tf_op jit(solution)/shard_map/all_to_all | solution.py:264
  1123.5 3.8 copy-start.38
  1131.1 51.9 %copy-start.12 = (f32[2,4,80,640]{3,2,1,0:T(8,128)S(1)}, f32[2,4,80,640]{3,2,1,0:T(8,128)}, u32[]{:S(2)}) copy-start(f32[2,4,80,640]{3,2,1,0:T(8,128)} %copy-done.10) | copy-start | bytes 4915204
  1131.1 51.9 %copy-start.19 = (f32[80,640]{1,0:T(8,128)S(1)}, f32[80,640]{1,0:T(8,128)}, u32[]{:S(2)}) copy-start(f32[80,640]{1,0:T(8,128)} %copy-done.17) | copy-start | bytes 614404
  1191.3 57.3 %all-to-all-start.8 = ((f32[2,4,80,640]{2,1,0,3:T(4,128)}), f32[2,4,80,640]{2,1,0,3:T(4,128)S(1)}, u32[]{:S(2)}, u32[]{:S(2)}) async-start(f32[2,4,80,640]{2,1,0,3:T(4,128)} %copy.204), calls=%async_computation.8 | async-start | bytes 5242880 | tf_op jit(solution)/shard_map/all_to_all | solution.py:324
  1248.5 1.5 copy-start.13
  1250.0 6.7 copy-start.9
  1264.5 6.0 copy-start.41
  1264.5 6.0 copy-start.42
  1264.5 30.5 %all-to-all-start.9 = ((f32[2,4,80,640]{2,1,0,3:T(4,128)}), f32[2,4,80,640]{2,1,0,3:T(4,128)}, u32[]{:S(2)}, u32[]{:S(2)}) async-start(f32[2,4,80,640]{2,1,0,3:T(4,128)} %copy.209), calls=%async_computation.9 | async-start | bytes 5242880 | tf_op jit(solution)/shard_map/all_to_all | solution.py:324
  1269.2 3.2 copy-start.14
  1299.0 2.8 copy-start.28
  1299.0 2.8 copy-start.29
  1305.6 2.3 copy-start
  1310.9 33.9 %all-to-all-start.10 = ((f32[2,16,80,160]{3,2,0,1:T(8,128)}), f32[2,16,80,160]{3,2,0,1:T(8,128)S(1)}, u32[]{:S(2)}, u32[]{:S(2)}) async-start(f32[2,16,80,160]{3,2,0,1:T(8,128)} %copy.214), calls=%async_computation.10 | async-start | bytes 5242880 | tf_op jit(solution)/shard_map/all_to_all | solution.py:338
  1344.8 34.7 %all-to-all-start.11 = ((f32[2,16,80,160]{3,2,0,1:T(8,128)}), f32[2,16,80,160]{3,2,0,1:T(8,128)}, u32[]{:S(2)}, u32[]{:S(2)}) async-start(f32[2,16,80,160]{3,2,0,1:T(8,128)} %copy.217), calls=%async_computation.11 | async-start | bytes 5242880 | tf_op jit(solution)/shard_map/all_to_all | solution.py:338
where the time goes:
time: 1400 us; the launch traced here: 1390 us
  waiting for transfers between devices  496 us (35%)
  Pallas kernels  469 us (34%)
  local copies, waits for them, and re-layouts  186 us (13%)
  other arithmetic  101 us (7%)
  matrix products  70.5 us (5%)
  starting transfers between devices  56.2 us (4%)
    pallas_call x8, Pallas kernels, transform(): pl.pallas_call(functools.partial(transform_kernel, forward=forward), grid...  396 us
    all_to_all x4, waiting for transfers between devices, to_latitudes(): lax.all_to_all(at_lat, 'wave', split_axis=4, concat_axis=3, tiled=True)  247 us
    all_to_all x4, waiting for transfers between devices, to_waves(): lax.all_to_all(returned, 'wave', split_axis=2, concat_axis=3, tiled=True)  187 us
    pallas_call x1, Pallas kernels, legendre(): pl.pallas_call(table_kernel, grid=(slots // GROUP,), in_specs=[coefficien...  72.6 us
    add x10, local copies, waits for them, and re-layouts, ordered(): return array + 0.0 * token(earlier)[0, 0]  44 us
    all_to_all x2, waiting for transfers between devices, on_device(): lax.all_to_all(restored, 'lev', split_axis=1, concat_axis=3, tiled=True)  42.1 us
    add x14, other arithmetic, ordered(): return array + 0.0 * token(earlier)[0, 0]  40 us
    dot_general x4, matrix products, products(): jnp.einsum('flsr,sk->flrk', jnp.stack([zonal, merid]), trigonometric_tabl...  35.2 us
  transfers between devices with their start and end apart: 12, of which 11 were waited for; matrix products, arithmetic and copies ran while one was open for 10% of the time, Pallas kernels for 14%

commit v1 on v0

--- a/solution.py
+++ b/solution.py
@@ -7,6 +7,7 @@
 from jax.experimental import pallas as pl
 from jax.experimental.pallas import tpu as pltpu
 from jax.sharding import PartitionSpec as P
+import numpy as np
 
 M = 640
 LAT = 640
@@ -341,6 +342,462 @@
     return (advanced, stream)
 
 
+def order_list(size):
+    blocks = size // (2 * GROUP)
+    first = np.arange(blocks // 2)[:, None, None]
+    block = np.concatenate([first, blocks - 1 - first], axis=1)
+    return (block * GROUP + np.arange(GROUP)[None, None, :]).astype(np.int32)
+
+
+def packed_width(size):
+    width = size + 2 * GROUP
+    return width, -(-width // LANES) * LANES
+
+
+def packed_coupling(parity, size):
+    width, lanes = packed_width(size)
+    orders = 2 * jnp.asarray(order_list(size)) + parity
+    lane = lax.broadcasted_iota(jnp.int32, (orders.shape[0], GROUP, lanes), 2)
+    split = size - 2 * GROUP * lax.broadcasted_iota(jnp.int32, lane.shape, 0)
+    wave = jnp.where(lane < split, orders[:, 0, :, None], orders[:, 1, :, None])
+    degree = wave + jnp.where(lane < split, lane, lane - split)
+    live = (degree < size) & (lane < width)
+    ahead_live = (degree + 1 < size) & (lane < width)
+    wave, degree = wave.astype(jnp.float32), degree.astype(jnp.float32)
+    square = wave * wave
+    following = degree + 1.0
+    here = jnp.sqrt((degree * degree - square) / (4.0 * degree * degree - 1.0))
+    beyond = jnp.sqrt((following * following - square) / (4.0 * following * following - 1.0))
+    lower = jnp.where(live, -(degree - 1.0) * here, 0.0)
+    upper = jnp.where(ahead_live, (degree + 2.0) * beyond, 0.0)
+    ahead = jnp.sqrt(
+        (4.0 * following * following - 1.0) / (following * following - square)
+    )
+    return lower, upper, live.astype(jnp.float32), ahead, here
+
+
+def half_table_kernel(coefficient_ref, start_ref, cos_ref, high_ref, low_ref, *, size):
+    lats = cos_ref.shape[1]
+    pair = pl.program_id(0)
+    spans = [(k, min(LANES, lats - k)) for k in range(0, lats, LANES)]
+    mus = [jnp.broadcast_to(cos_ref[0:1, k : k + n], (GROUP, n)) for k, n in spans]
+    blocks = coefficient_ref.shape[1]
+    restart = size // 16 - pair
+
+    def fresh(which, k, n):
+        return (
+            jnp.zeros((GROUP, n), jnp.float32),
+            jnp.ones((GROUP, n), jnp.float32),
+            start_ref[0, which, :, k : k + n],
+        )
+
+    def block(index, carry):
+        first = pl.multiple_of(index * 16, 16)
+        again = index == restart
+        coefficients = coefficient_ref[0, index]
+        ahead = [jnp.broadcast_to(coefficients[:, t : t + 1], (GROUP, LANES)) for t in range(16)]
+        behind = [
+            jnp.broadcast_to(coefficients[:, 16 + t : 17 + t], (GROUP, LANES)) for t in range(16)
+        ]
+        following_carry = []
+        for (k, n), mu, old in zip(spans, mus, carry):
+            previous, current, log_scale = [
+                jnp.where(again, new, kept) for new, kept in zip(fresh(1, k, n), old)
+            ]
+            rows = []
+            for t in range(16):
+                if t % 8 == 0:
+                    scale = jnp.exp(log_scale)
+                rows.append(current * scale)
+                following = ahead[t][:, :n] * (mu * current - behind[t][:, :n] * previous)
+                previous, current = current, following
+                if t % 8 == 7:
+                    magnitude = jnp.abs(previous) + jnp.abs(current)
+                    inverse = 1.0 / magnitude
+                    previous, current = previous * inverse, current * inverse
+                    log_scale = log_scale + jnp.log(magnitude)
+            following_carry.append((previous, current, log_scale))
+            values = jnp.concatenate(
+                [
+                    jnp.swapaxes(jnp.stack(rows[:8]), 0, 1),
+                    jnp.swapaxes(jnp.stack(rows[8:]), 0, 1),
+                ],
+                axis=1,
+            )
+            high = values.astype(jnp.bfloat16)
+            high_ref[0, :, pl.ds(first, 16), k : k + n] = high
+            low_ref[0, :, pl.ds(first, 16), k : k + n] = (
+                values - high.astype(jnp.float32)
+            ).astype(jnp.bfloat16)
+        return tuple(following_carry)
+
+    lax.fori_loop(0, blocks, block, tuple(fresh(0, k, n) for k, n in spans))
+
+
+def half_table(parity, cosines, sines, ahead, behind, size):
+    width, _ = packed_width(size)
+    orders = 2 * jnp.asarray(order_list(size)) + parity
+    pairs, lats = orders.shape[0], cosines.shape[0]
+    wavenum = orders.reshape(-1).astype(jnp.float32)[:, None]
+    counter = jnp.arange(1, size, dtype=jnp.int32).astype(jnp.float32)
+    halves = 0.5 * jnp.log((2.0 * counter + 1.0) / (2.0 * counter))
+    start_log = jnp.sum(jnp.where(counter[None, :] <= wavenum, halves[None, :], 0.0), axis=1)
+    log_start = -0.5 * math.log(2.0) + start_log[:, None] + wavenum * jnp.log(sines)[None, :]
+    log_start = log_start.reshape(pairs, 2, GROUP, lats)
+    blocks = width // 16
+
+    def by_block(array):
+        return jnp.swapaxes(array[:, :, :width].reshape(pairs, GROUP, blocks, 16), 1, 2)
+
+    coefficients = jnp.concatenate([by_block(ahead), by_block(behind)], axis=3)
+    table = jax.ShapeDtypeStruct((pairs, GROUP, width, lats), jnp.bfloat16)
+    table_spec = pl.BlockSpec((1, GROUP, width, lats), lambda g: (g, 0, 0, 0))
+    return pl.pallas_call(
+        functools.partial(half_table_kernel, size=size),
+        grid=(pairs,),
+        in_specs=[
+            pl.BlockSpec((1, blocks, GROUP, 32), lambda g: (g, 0, 0, 0)),
+            pl.BlockSpec((1, 2, GROUP, lats), lambda g: (g, 0, 0, 0)),
+            pl.BlockSpec((1, lats), lambda g: (0, 0)),
+        ],
+        out_specs=[table_spec, table_spec],
+        out_shape=[table, table],
+        compiler_params=pltpu.CompilerParams(vmem_limit_bytes=VMEM),
+        cost_estimate=pl.CostEstimate(
+            flops=pairs * GROUP * width * lats * 10,
+            bytes_accessed=pairs * GROUP * width * lats * 4,
+            transcendentals=0,
+        ),
+        name="half_table",
+    )(coefficients, log_start, cosines[None, :])
+
+
+def split_halves(value):
+    high = value.astype(jnp.bfloat16)
+    return high, (value - high.astype(jnp.float32)).astype(jnp.bfloat16)
+
+
+def visit_kernel(*refs, size, stage):
+    refs = list(refs)
+    high_ref, low_ref = refs.pop(0), refs.pop(0)
+    pair = pl.program_id(0)
+    width, lanes = packed_width(size)
+    split = size - 2 * GROUP * pair
+    lats = high_ref.shape[3]
+    position = lax.broadcasted_iota(jnp.int32, (1, lanes), 1)
+    in_first, even = position < split, position % 2 == 0
+    picks = [in_first & even, in_first & ~even, ~in_first & even, ~in_first & ~even]
+    step = TIME_STEP / size
+
+    def multiply(fields, table_slot, chunks, contract):
+        rows = fields.shape[0]
+        field_high, field_low = split_halves(fields)
+        both_fields = jnp.concatenate([field_high, field_low], axis=0)
+        both = small = None
+        dims = (((1,), (contract,)), ((), ()))
+        for c0, c1 in chunks:
+            table_high = high_ref[0, table_slot, c0:c1, :]
+            table_low = low_ref[0, table_slot, c0:c1, :]
+            if contract == 0:
+                left, left_high = both_fields[:, c0:c1], field_high[:, c0:c1]
+            else:
+                left, left_high = both_fields, field_high
+            part = lax.dot_general(left, table_high, dims, preferred_element_type=jnp.float32)
+            part_small = lax.dot_general(
+                left_high, table_low, dims, preferred_element_type=jnp.float32
+            )
+            if both is None:
+                both, small = [part], [part_small]
+            elif contract == 0:
+                both, small = [both[0] + part], [small[0] + part_small]
+            else:
+                both, small = both + [part], small + [part_small]
+        both = jnp.concatenate(both, axis=1) if len(both) > 1 else both[0]
+        small = jnp.concatenate(small, axis=1) if len(small) > 1 else small[0]
+        return both[:rows] + (both[rows:] + small)
+
+    chunks = [(c0, min(c0 + 256, width)) for c0 in range(0, width, 256)]
+
+    if stage != "last":
+        lower_ref, upper_ref = refs.pop(0), refs.pop(0)
+    live_ref = refs.pop(0)
+    if stage == "first":
+        own_q_ref, other_q_ref, start_ref, own_ref, other_ref, fields, firsts, seconds = refs
+        padding = jnp.zeros((4, lanes - size), jnp.float32)
+        fields[0] = jnp.swapaxes(own_q_ref[:, 0, 0], 0, 1)
+        fields[1] = jnp.swapaxes(other_q_ref[:, 0, 0], 0, 1)
+        fields[2] = jnp.swapaxes(own_q_ref[:, 0, 1], 0, 1)
+        fields[3] = jnp.swapaxes(other_q_ref[:, 0, 1], 0, 1)
+    elif stage == "middle":
+        own_b_ref, other_b_ref, start_ref, rate_ref, own_ref, other_ref, fields, firsts, seconds = refs
+    else:
+        own_b_ref, other_b_ref, start_ref, rate_ref, own_ref, other_ref, fields, firsts, seconds = refs
+    if stage != "first":
+        fields[0] = jnp.swapaxes(own_b_ref[:, 0, 0], 0, 1)
+        fields[1] = jnp.swapaxes(other_b_ref[:, 0, 0], 0, 1)
+        fields[2] = jnp.swapaxes(own_b_ref[:, 0, 1], 0, 1)
+        fields[3] = jnp.swapaxes(other_b_ref[:, 0, 1], 0, 1)
+
+    def one_slot(slot, carry):
+        live = live_ref[0, pl.ds(slot, 1), :]
+        block_a = jnp.concatenate([fields[0, slot], fields[1, slot]], axis=0)
+        block_b = jnp.concatenate([fields[2, slot], fields[3, slot]], axis=0)
+        if stage == "first":
+            block_a = jnp.concatenate([block_a, padding], axis=1)
+            block_b = pltpu.roll(jnp.concatenate([block_b, padding], axis=1), split, 1)
+            spectra = jnp.where(in_first, block_a, block_b) * live
+            start_ref[0, slot] = spectra
+        else:
+            sides = []
+            for block in (block_a, block_b):
+                north, south = block[:, :lats], block[:, lats:]
+                sides += [north + south, north - south]
+            sums = multiply(jnp.concatenate(sides, axis=0), slot, chunks, 1)
+            sums = jnp.concatenate(
+                [sums, jnp.zeros((sums.shape[0], lanes - width), jnp.float32)], axis=1
+            )
+            rate = jnp.zeros((4, lanes), jnp.float32)
+            for index, pick in enumerate(picks):
+                rate = jnp.where(pick, sums[4 * index : 4 * index + 4], rate)
+            rate = rate * live
+            if stage == "middle":
+                rate_ref[0, slot] = rate
+                spectra = start_ref[0, slot] + step * rate
+            else:
+                spectra = start_ref[0, slot] + 0.5 * step * (rate_ref[0, slot] + rate)
+        if stage == "last":
+            firsts[slot, :4] = jnp.where(in_first, spectra, 0.0)[:, :size]
+            turned = pltpu.roll(spectra, lanes - split, 1)
+            seconds[slot, :4] = jnp.where(position < width - split, turned, 0.0)[:, :size]
+        else:
+            meridional = lower_ref[0, pl.ds(slot, 1), :] * pltpu.roll(
+                spectra, 1, 1
+            ) + upper_ref[0, pl.ds(slot, 1), :] * pltpu.roll(spectra, lanes - 1, 1)
+            both = jnp.concatenate([spectra, meridional], axis=0)
+            masked = jnp.concatenate([jnp.where(pick, both, 0.0) for pick in picks], axis=0)
+            sums = multiply(masked, slot, chunks, 0)
+            firsts[slot] = jnp.concatenate([sums[0:8] + sums[8:16], sums[0:8] - sums[8:16]], axis=1)
+            seconds[slot] = jnp.concatenate(
+                [sums[16:24] + sums[24:32], sums[16:24] - sums[24:32]], axis=1
+            )
+        return carry
+
+    lax.fori_loop(0, GROUP, one_slot, 0)
+    for which, result in ((0, firsts), (1, seconds)):
+        turned = jnp.swapaxes(result[...], 0, 1)
+        if stage == "last":
+            own_ref[:, 0, which] = turned[0:2]
+            other_ref[:, 0, which] = turned[2:4]
+        else:
+            own_ref[0:2, 0, which] = turned[0:2]
+            own_ref[2:4, 0, which] = turned[4:6]
+            other_ref[0:2, 0, which] = turned[2:4]
+            other_ref[2:4, 0, which] = turned[6:8]
+
+
+def visit(stage, table, tables, arrays, size):
+    width, lanes = packed_width(size)
+    pairs, lats = table[0].shape[0], table[0].shape[3]
+    table_spec = pl.BlockSpec((1, GROUP, width, lats), lambda g: (g, 0, 0, 0))
+    row_spec = pl.BlockSpec((1, GROUP, lanes), lambda g: (g, 0, 0))
+    packed_spec = pl.BlockSpec((1, GROUP, 4, lanes), lambda g: (g, 0, 0, 0))
+    packed = jax.ShapeDtypeStruct((pairs, GROUP, 4, lanes), jnp.float32)
+
+    def slots_spec(rows, columns):
+        return pl.BlockSpec((rows, 1, 2, GROUP, columns), lambda g: (0, g, 0, 0, 0))
+
+    def slots_shape(rows, columns):
+        return jax.ShapeDtypeStruct((rows, pairs, 2, GROUP, columns), jnp.float32)
+
+    at_lat = [slots_spec(4, 2 * lats)] * 2
+    at_lat_shape = [slots_shape(4, 2 * lats)] * 2
+    if stage == "first":
+        in_columns, out_columns, out_rows = size, 2 * lats, 8
+        specs = [row_spec] * 3 + [slots_spec(2, size)] * 2
+        out_specs, out_shape = [packed_spec] + at_lat, [packed] + at_lat_shape
+    elif stage == "middle":
+        in_columns, out_columns, out_rows = 2 * lats, 2 * lats, 8
+        specs = [row_spec] * 3 + [slots_spec(2, 2 * lats)] * 2 + [packed_spec]
+        out_specs, out_shape = [packed_spec] + at_lat, [packed] + at_lat_shape
+    else:
+        in_columns, out_columns, out_rows = 2 * lats, size, 4
+        specs = [row_spec] + [slots_spec(2, 2 * lats)] * 2 + [packed_spec] * 2
+        out_specs, out_shape = [slots_spec(2, size)] * 2, [slots_shape(2, size)] * 2
+    return pl.pallas_call(
+        functools.partial(visit_kernel, size=size, stage=stage),
+        grid=(pairs,),
+        in_specs=[table_spec] * 2 + specs,
+        out_specs=out_specs,
+        out_shape=out_shape,
+        scratch_shapes=[
+            pltpu.VMEM((4, GROUP, 2, in_columns), jnp.float32),
+            pltpu.VMEM((GROUP, out_rows, out_columns), jnp.float32),
+            pltpu.VMEM((GROUP, out_rows, out_columns), jnp.float32),
+        ],
+        compiler_params=pltpu.CompilerParams(vmem_limit_bytes=VMEM),
+        cost_estimate=pl.CostEstimate(
+            flops=pairs * GROUP * width * lats * 200,
+            bytes_accessed=pairs * GROUP * width * lats * 4,
+            transcendentals=0,
+        ),
+        name="visit_" + stage,
+    )(*table, *tables, *arrays)
+
+
+def by_level(vorticity, wind_lam, wind_mu, modes, mode_rates, wave_order, lat_order):
+    comps, levels, slots, size = vorticity.shape
+    lat_slots, longitudes = wind_lam.shape[1:]
+    lats = lat_order.shape[0]
+    half_lats, half_lons = lats // 2, longitudes // 2
+    devices = levels
+    wave_pos = lax.axis_index("wave")
+    lev_pos = lax.axis_index("lev")
+    parity = wave_pos % 2
+    swap = [(d, d ^ 1) for d in range(devices)]
+
+    def exchange(array):
+        return lax.ppermute(array, "wave", swap)
+
+    def to_levels(array):
+        return lax.all_to_all(array, "wave", split_axis=0, concat_axis=0, tiled=True)
+
+    every = jnp.arange(size, dtype=jnp.int32)
+    slot_of = jnp.zeros((size,), jnp.int32).at[wave_order].set(every)
+    lat_slot_of = jnp.zeros((lats,), jnp.int32).at[lat_order].set(
+        jnp.arange(lats, dtype=jnp.int32)
+    )
+    order = order_list(size)
+    pairs = order.shape[0]
+    flat_order = jnp.asarray(order.reshape(-1))
+
+    spread = to_levels(jnp.swapaxes(vorticity, 0, 1)).reshape(devices * comps * slots, size)
+
+    def rows_of(which):
+        slot = jnp.take(slot_of, 2 * flat_order + which)
+        row = (slot // slots) * (comps * slots) + slot % slots
+        rows = jnp.take(spread, jnp.concatenate([row, row + slots]), axis=0)
+        return rows.reshape(comps, pairs, 2, GROUP, size)
+
+    north = jnp.arange(half_lats, dtype=jnp.int32)
+    cosines, sines, weights = latitudes(north)
+    lower, upper, live, ahead, behind = packed_coupling(parity, size)
+    table = half_table(parity, cosines, sines, ahead, behind, size)
+
+    lat_rows = jnp.take(lat_slot_of, jnp.concatenate([north, lats - 1 - north]))
+
+    def wind_of(wind):
+        rows = to_levels(wind).reshape(lats, longitudes)
+        return jnp.take(rows, lat_rows, axis=0)
+
+    sign = 1.0 - 2.0 * parity.astype(jnp.float32)
+    row_scale = jnp.concatenate([weights, weights])[:, None] / longitudes
+
+    def trigonometric(which):
+        waves = 2 * flat_order + which
+        phase = waves[:, None] * jnp.arange(half_lons, dtype=jnp.int32)[None, :] % longitudes
+        angles = 2.0 * math.pi / longitudes * phase.astype(jnp.float32)
+        cos, sin = jnp.cos(angles), jnp.sin(angles)
+        double = jnp.where(waves == 0, 1.0, 2.0).astype(jnp.float32)[:, None]
+        scaled = double * waves.astype(jnp.float32)[:, None]
+        zonal = jnp.concatenate([-scaled * sin, -scaled * cos], axis=0)
+        merid = jnp.concatenate([double * cos, -double * sin], axis=0)
+        back = jnp.concatenate([cos, -sin], axis=0)
+        return zonal, merid, back
+
+    trig_own, trig_other = trigonometric(parity), trigonometric(1 - parity)
+
+    def tendency_rows(own, other, wind_l, wind_m):
+        received = exchange(other)
+
+        def grid(field, table_own, table_other):
+            mine = own[2 * field : 2 * field + 2].reshape(size, lats)
+            theirs = received[2 * field : 2 * field + 2].reshape(size, lats)
+            here = jnp.einsum("sr,sk->rk", mine, table_own, precision=HIGH_ACCURACY)
+            there = jnp.einsum("sr,sk->rk", theirs, table_other, precision=HIGH_ACCURACY)
+            return here + there, sign * (here - there)
+
+        lam_near, lam_far = grid(0, trig_own[0], trig_other[0])
+        mu_near, mu_far = grid(1, trig_own[1], trig_other[1])
+        near = -(wind_l[:, :half_lons] * lam_near + wind_m[:, :half_lons] * mu_near) * row_scale
+        far = -(wind_l[:, half_lons:] * lam_far + wind_m[:, half_lons:] * mu_far) * row_scale
+        far = sign * far
+
+        def back(folded, table_back):
+            rows = jnp.einsum("zk,rk->zr", table_back, folded, precision=HIGH_ACCURACY)
+            return rows.reshape(comps, pairs, 2, GROUP, lats)
+
+        other_rows = exchange(back(near - far, trig_other[2]))
+        own_rows = back(near + far, trig_own[2])
+        return own_rows, other_rows
+
+    own_q, other_q = rows_of(parity), exchange(rows_of(1 - parity))
+    start, own_a, other_a = visit("first", table, [lower, upper, live], [own_q, other_q], size)
+    wind_l, wind_m = wind_of(wind_lam), wind_of(wind_mu)
+    own_b, other_b = tendency_rows(own_a, other_a, wind_l, wind_m)
+    first_rate, own_a, other_a = visit(
+        "middle", table, [lower, upper, live], [own_b, other_b, start], size
+    )
+    own_b, other_b = tendency_rows(own_a, other_a, wind_l, wind_m)
+    own_q, other_q = visit("last", table, [live], [own_b, other_b, start, first_rate], size)
+
+    received = exchange(other_q)
+    stacked = jnp.concatenate(
+        [own_q.reshape(comps * size // 2, size), received.reshape(comps * size // 2, size)], axis=0
+    )
+    place = jnp.zeros((size // 2,), jnp.int32).at[flat_order].set(
+        jnp.arange(size // 2, dtype=jnp.int32)
+    )
+    wave_rows = wave_order.reshape(devices, 1, slots)
+    row = jnp.take(place, wave_rows // 2)
+    row = row + jnp.where(wave_rows % 2 == parity, 0, comps * size // 2)
+    row = row + (size // 2) * jnp.arange(comps, dtype=jnp.int32)[None, :, None]
+    leaving = jnp.take(stacked, row.reshape(-1), axis=0).reshape(devices, comps * slots, size)
+    advanced = to_levels(leaving)
+
+    lev_count = modes.shape[0] // levels
+    rows_each = comps * slots // lev_count
+    pieces = advanced.reshape(levels, lev_count, rows_each, size)
+    gathered = lax.all_to_all(pieces, "lev", split_axis=1, concat_axis=0, tiled=True)
+    gathered = gathered.reshape(levels * lev_count, rows_each, size)
+    projected = jnp.einsum("lk,lrj->krj", modes, gathered, precision=HIGH_ACCURACY)
+    waves = lax.dynamic_slice_in_dim(wave_order, wave_pos * slots, slots)
+    block_waves = jnp.take(
+        waves, (lev_pos * rows_each + jnp.arange(rows_each, dtype=jnp.int32)) % slots
+    )
+    degree = (block_waves[:, None] + every[None, :]).astype(jnp.float32)
+    kappa = degree * (degree + 1.0) / (size * (size + 1.0))
+    projected = projected / (kappa[None] + mode_rates[:, None, None])
+    restored = jnp.einsum("lk,krj->lrj", modes, projected, precision=HIGH_ACCURACY)
+    restored = restored * (degree < size - 0.5).astype(jnp.float32)
+    stream = lax.all_to_all(
+        restored.reshape(lev_count, levels, rows_each, size), "lev", split_axis=0, concat_axis=0, tiled=True
+    )
+    stream = jnp.moveaxis(stream.reshape(lev_count, levels, rows_each, size), 0, 1)
+    stream = stream.reshape(levels, comps, slots, size)
+    return (
+        jnp.swapaxes(advanced.reshape(levels, comps, slots, size), 0, 1),
+        jnp.swapaxes(stream, 0, 1),
+    )
+
+
+def on_any(vorticity, wind_lam, wind_mu, modes, mode_rates, wave_order, lat_order):
+    comps, levels, slots, size = vorticity.shape
+    devices = wave_order.shape[0] // slots
+    lats, longitudes = lat_order.shape[0], wind_lam.shape[2]
+    rows = comps * slots
+    whole = (
+        levels == devices
+        and devices % 2 == 0
+        and size == wave_order.shape[0]
+        and size % (4 * GROUP) == 0
+        and lats % 2 == 0
+        and longitudes % 2 == 0
+        and rows % (modes.shape[0] // levels) == 0
+    )
+    take = by_level if whole else on_device
+    return take(vorticity, wind_lam, wind_mu, modes, mode_rates, wave_order, lat_order)
+
+
 def solution(mesh):
     placed = (
         P(None, "lev", "wave", None),
@@ -352,7 +809,7 @@
         P(),
     )
     return jax.shard_map(
-        on_device,
+        on_any,
         mesh=mesh,
         in_specs=placed,
         out_specs=(P(None, "lev", "wave", None), P(None, "lev", "wave", None)),

time: 1400 us -> 1000 us (0.71)
  waiting for transfers between devices: 496 us -> 142 us
  blocking collectives: 0 us -> 159 us
  local copies, waits for them, and re-layouts: 186 us -> 89.3 us
  other arithmetic: 101 us -> 36.5 us
  Pallas kernels: 469 us -> 506 us
  starting transfers between devices: 56.2 us -> 19.7 us
  matrix products: 70.5 us -> 40.7 us
    all_to_all x12 -> x4, waiting for transfers between devices: 496 us -> 142 us  [the longest x2 70.5 us: to_levels(): lax.all_to_all(array, 'wave', split_axis=0, concat_axis=0, tiled=True)]
    all_to_all x0 -> x2, blocking collectives: none -> 159 us  [to_levels(): lax.all_to_all(array, 'wave', split_axis=0, concat_axis=0, tiled=True)]
    all_to_all x23 -> x1, local copies, waits for them, and re-layouts: 79.2 us -> 2.17 us  [by_level(): lax.all_to_all(restored.reshape(lev_count, levels, rows_each, size), 'lev...]
    add x19 -> x5, other arithmetic: 46.3 us -> 1.05 us  [the longest x2 0.93 us: half_table(): -0.5 * math.log(2.0) + start_log[:, None]]
    add x10 -> x6, local copies, waits for them, and re-layouts: 44 us -> 0.42 us  [the longest x5 0.32 us: by_level(): row = row + size // 2 * jnp.arange(comps, dtype=jnp.int32)[None, :, None]]
    gather x0 -> x11, local copies, waits for them, and re-layouts: none -> 38.3 us  [the longest x2 11.2 us: wind_of(): return jnp.take(rows, lat_rows, axis=0)]
    all_to_all x12 -> x4, starting transfers between devices: 56.2 us -> 17.9 us  [the longest x2 8.28 us: to_levels(): lax.all_to_all(array, 'wave', split_axis=0, concat_axis=0, tiled=True)]
    pallas_call x9 -> x4, Pallas kernels: 469 us -> 506 us  [the longest x3 343 us: visit(): pl.pallas_call(functools.partial(visit_kernel, size=size, stage=stage), g...]
  transfers between devices with their start and end apart: 12 -> 10, of which waited for: 11 -> 3; matrix products, arithmetic and copies ran while one was open for 10% -> 11% of each run, Pallas kernels for 14% -> 25%
where the time goes in v1:
time: 1000 us; the launch traced here: 996 us
  Pallas kernels  506 us (51%)
  blocking collectives  159 us (16%)
  waiting for transfers between devices  142 us (14%)
  local copies, waits for them, and re-layouts  89.3 us (9%)
  matrix products  40.7 us (4%)
  other arithmetic  36.5 us (4%)
  starting transfers between devices  19.7 us (2%)
    pallas_call x3, Pallas kernels, visit(): pl.pallas_call(functools.partial(visit_kernel, size=size, stage=stage), g...  343 us
    pallas_call x1, Pallas kernels, half_table(): pl.pallas_call(functools.partial(half_table_kernel, size=size), grid=(pai...  163 us
    all_to_all x2, blocking collectives, to_levels(): lax.all_to_all(array, 'wave', split_axis=0, concat_axis=0, tiled=True)  159 us
    all_to_all x2, waiting for transfers between devices, to_levels(): lax.all_to_all(array, 'wave', split_axis=0, concat_axis=0, tiled=True)  70.5 us
    all_to_all x1, waiting for transfers between devices, by_level(): lax.all_to_all(pieces, 'lev', split_axis=1, concat_axis=0, tiled=True)  36.5 us
    all_to_all x1, waiting for transfers between devices, by_level(): lax.all_to_all(restored.reshape(lev_count, levels, rows_each, size), 'lev...  35.2 us
  transfers between devices with their start and end apart: 10, of which 3 were waited for; matrix products, arithmetic and copies ran while one was open for 11% of the time, Pallas kernels for 25%

profile of v1, /device:TPU:0, one launch (start us, length us, event | category | flops | bytes accessed | tf_op | source)
XLA Modules:
  0.0 995.9 jit_solution(3535716360871183524)
XLA Ops:
  0.6 2.2 copy.71
  2.8 80.6 %all_to_all.40 = f32[8,2,80,640]{3,2,1,0:T(8,128)} all-to-all(f32[8,2,80,640]{3,2,1,0:T(8,128)S(1)} %bitcast.81), channel_id=1, replica_groups=mesh['lev'=4,'wave'=8] {'wave'}, dimensions={0} | all-to-all | bytes 6553600 | tf_op jit(solution)/shard_map/all_to_all | solution.py:662
  83.4 3.8 all-to-all-start
  87.9 2.0 multiply_select_fusion
  90.0 0.9 fusion.49
  90.9 70.5 %all-to-all-done = f32[8,80,1280]{2,1,0:T(8,128)S(1)} async-done(((f32[8,80,1280]{2,1,0:T(8,128)}), f32[8,80,1280]{2,1,0:T(8,128)S(1)}, u32[]{:S(2)}, u32[]{:S(2)}) %all-to-all-start) | async-done | bytes 3276832 | tf_op jit(solution)/shard_map/all_to_all | solution.py:662
  161.4 4.5 all-to-all-start.2
  165.9 3.8 reshape.652
  169.7 3.7 reshape.653
  173.6 4.1 scatter_custom_fusion.1
  177.7 1.7 gather_fusion.5
  179.4 1.7 gather_fusion.7
  181.1 4.3 scatter_custom_fusion
  185.6 2.8 gather_fusion.1
  188.6 9.0 copy_bitcast_fusion
  197.5 5.5 gather_fusion.8
  203.1 2.8 broadcast_select_fusion.3
  206.9 5.6 pad_maximum_fusion.coefficient_ref
  212.6 0.9 multiply_add_fusion.start_ref
  213.5 162.9 %half_table.1 = (bf16[20,8,656,320]{3,2,1,0:T(8,128)(2,1)}, bf16[20,8,656,320]{3,2,1,0:T(8,128)(2,1)}) custom-call(f32[20,41,8,32]{3,2,1,0:T(8,128)} %pad_maximum_fusion.coefficient_ref, f32[20,2,8,320]{3,2,1,0:T(8,128)} %multiply_add_fusion.start_ref, f32[1,320]{1,0:T(1,128)} %multiply_cosine_fusion.cos_ref), custom_call_target="tpu_custom_call" | custom-call | flops 335872000 | bytes 134348800 | tf_op jit(solution)/shard_map/half_table/pallas_call | solution.py:455
  376.6 1.0 fusion.53.refs_4_.refs_2_
  377.6 5.5 gather_fusion.6
  383.1 2.8 broadcast_select_fusion.4
  385.9 83.2 %visit_first.1 = (f32[20,8,4,768]{3,2,1,0:T(4,128)}, f32[4,20,2,8,640]{4,3,2,1,0:T(8,128)}, f32[4,20,2,8,640]{4,3,2,1,0:T(8,128)}) custom-call(bf16[20,8,656,320]{3,2,1,0:T(8,128)(2,1)} %get-tuple-element.15.refs_0_, bf16[20,8,656,320]{3,2,1,0:T(8,128)(2,1)} %get-tuple-element.16.refs_1_, f32[20,8,768]{2,1,0:T(8,128)} %get-tuple-element.52.refs_2_, ...), custom_call_target="tpu_custom_call" | custom-call | flops 6717440000 | bytes 134348800 | tf_op jit(solution)/shard_map/visit_first/pallas_call | solution.py:626
  469.5 5.2 fusion.28
  474.7 5.2 fusion.36
  479.9 3.7 gather_fusion.4
  483.6 7.5 gather_fusion.9
  491.1 3.6 broadcast_select_fusion.1
  495.2 1.5 copy-done.19
  497.2 2.6 fusion.21
  499.9 2.6 fusion.17
  502.6 2.3 fusion.102
  504.9 2.6 fusion.19
  507.6 3.5 multiply_multiply_fusion.1
  511.2 2.7 fusion.10
  514.3 3.5 fusion.12
  517.8 166.6 %visit_middle.1 = (f32[20,8,4,768]{3,2,1,0:T(4,128)}, f32[4,20,2,8,640]{4,3,2,1,0:T(8,128)}, f32[4,20,2,8,640]{4,3,2,1,0:T(8,128)}) custom-call(bf16[20,8,656,320]{3,2,1,0:T(8,128)(2,1)} %get-tuple-element.15.refs_0_, bf16[20,8,656,320]{3,2,1,0:T(8,128)(2,1)} %get-tuple-element.16.refs_1_, f32[20,8,768]{2,1,0:T(8,128)} %get-tuple-element.52.refs_2_, ...), custom_call_target="tpu_custom_call" | custom-call | flops 6717440000 | bytes 134348800 | tf_op jit(solution)/shard_map/visit_middle/pallas_call | solution.py:626
  684.5 2.3 fusion.101
  686.9 2.6 fusion.20
  689.6 2.6 fusion.16
  693.6 2.6 fusion.18
  696.3 3.5 multiply_multiply_fusion
  699.8 2.7 fusion.6
  703.0 3.6 fusion.8
  706.6 1.2 copy-done.29
  707.7 93.4 %visit_last.1 = (f32[2,20,2,8,640]{4,3,2,1,0:T(8,128)}, f32[2,20,2,8,640]{4,3,2,1,0:T(8,128)}) custom-call(bf16[20,8,656,320]{3,2,1,0:T(8,128)(2,1)} %get-tuple-element.15.refs_0_, bf16[20,8,656,320]{3,2,1,0:T(8,128)(2,1)} %get-tuple-element.16.refs_1_, f32[20,8,768]{2,1,0:T(8,128)} %fusion.53.refs_4_.refs_2_, f32[2,20,2,8,640]{4,3,2,1,0:T(8,128)} %bitcast.92, ...), custom_call_target="tpu_custom_call" | custom-call | flops 6717440000 | bytes 134348800 | tf_op jit(solution)/shard_map/visit_last/pallas_call | solution.py:626
  801.8 4.3 gather_fusion
  806.7 1.2 copy-done.28
  807.9 2.1 pad_maximum_fusion.1
  810.0 4.8 gather_fusion.2
  814.8 2.2 broadcast_select_fusion.2
  817.0 78.9 %all_to_all.41 = f32[8,160,640]{2,1,0:T(8,128)S(1)} all-to-all(f32[8,160,640]{2,1,0:T(8,128)S(1)} %broadcast_select_fusion.2), channel_id=1, replica_groups=mesh['lev'=4,'wave'=8] {'wave'}, dimensions={0} | all-to-all | bytes 6553600 | tf_op jit(solution)/shard_map/all_to_all | solution.py:662
  895.9 1.9 copy.57
  897.8 5.0 all-to-all-start.4
  903.9 36.5 %all-to-all-done.4 = f32[8,4,40,640]{3,2,0,1:T(8,128)} async-done(((f32[8,4,40,640]{3,2,0,1:T(8,128)}), f32[8,4,40,640]{3,2,0,1:T(8,128)}, u32[]{:S(2)}, u32[]{:S(2)}) %all-to-all-start.4) | async-done | bytes 3276832 | tf_op jit(solution)/shard_map/all_to_all | solution.py:760
  940.4 3.7 fusion.1
  944.1 1.7 multiply_bitcast_fusion
  945.9 3.6 copy.60
  949.5 4.7 all-to-all-start.5
  954.2 1.9 copy.62
  956.1 35.2 %all-to-all-done.5 = f32[4,8,40,640]{3,2,1,0:T(8,128)} async-done(((f32[4,8,40,640]{3,2,1,0:T(8,128)}), f32[4,8,40,640]{3,2,1,0:T(8,128)}, u32[]{:S(2)}, u32[]{:S(2)}) %all-to-all-start.5) | async-done | bytes 3276832 | tf_op jit(solution)/shard_map/all_to_all | solution.py:772
  991.3 2.2 copy.61
  993.5 1.9 copy.63
  (147 shorter events, 8.6 us)
Async XLA Ops:
  0.6 939.8 %copy-start = (f32[32,32]{1,0:T(8,128)S(1)}, f32[32,32]{1,0:T(8,128)}, u32[]{:S(2)}) copy-start(f32[32,32]{1,0:T(8,128)} %param.19) | copy-start | bytes 12292
  83.4 3.8 copy-start.33
  83.4 4.5 copy-start.32
  83.4 4.5 copy-start.30
  83.4 78.0 %all-to-all-start = ((f32[8,80,1280]{2,1,0:T(8,128)}), f32[8,80,1280]{2,1,0:T(8,128)S(1)}, u32[]{:S(2)}, u32[]{:S(2)}) async-start(f32[8,80,1280]{2,1,0:T(8,128)} %param.17), calls=%async_computation | async-start | bytes 6553600 | tf_op jit(solution)/shard_map/all_to_all | solution.py:662
  161.4 322.2 %all-to-all-start.2 = ((f32[8,80,1280]{2,1,0:T(8,128)}), f32[8,80,1280]{2,1,0:T(8,128)}, u32[]{:S(2)}, u32[]{:S(2)}) async-start(f32[8,80,1280]{2,1,0:T(8,128)} %param.18), calls=%async_computation.2 | async-start | bytes 6553600 | tf_op jit(solution)/shard_map/all_to_all | solution.py:662
  177.7 3.4 copy-start.34
  205.9 180.1 %collective-permute-start = (f32[2,20,2,8,640]{4,3,2,1,0:T(8,128)}, f32[2,20,2,8,640]{4,3,2,1,0:T(8,128)}, u32[]{:S(2)}, u32[]{:S(2)}) collective-permute-start(f32[2,20,2,8,640]{4,3,2,1,0:T(8,128)} %bitcast.8), channel_id=1, source_target_pairs={{0,1},{1,0},{2,3},{3,2},{4,5},{5,4},{6,7},{7,6},{8,9},{9,8},{10,11... | collective-permute-start | bytes 4915208 | tf_op jit(solution)/shard_map/ppermute | solution.py:659
  469.1 33.4 %collective-permute-start.1 = (f32[4,20,2,8,640]{4,3,2,1,0:T(8,128)}, f32[4,20,2,8,640]{4,3,2,1,0:T(8,128)}, u32[]{:S(2)}, u32[]{:S(2)}) collective-permute-start(f32[4,20,2,8,640]{4,3,2,1,0:T(8,128)} %get-tuple-element.18), channel_id=1, source_target_pairs={{0,1},{1,0},{2,3},{3,2},{4,5},{5,4},{6,7},{7,6},{8,9},{9,8},{10,11... | collective-permute-start | bytes 9830408 | tf_op jit(solution)/shard_map/ppermute | solution.py:659
  491.1 3.9 copy-start.27
  494.7 12.9 %copy-start.2 = (f32[640,1280]{1,0:T(8,128)}, f32[640,1280]{1,0:T(8,128)S(1)}, u32[]{:S(2)}) copy-start(f32[640,1280]{1,0:T(8,128)S(1)} %get-tuple-element.89) | copy-start | bytes 9830404
  494.9 1.7 copy-start.19
  494.9 2.3 copy-start.21
  497.2 2.6 copy-start.15
  497.2 2.6 copy-start.17
  502.5 2.3 copy-start.11
  502.5 2.4 copy-start.13
  504.9 2.6 copy-start.23
  504.9 2.6 copy-start.25
  507.6 3.6 copy-start.4
  507.6 3.6 copy-start.5
  511.1 3.1 copy-start.7
  511.1 3.1 copy-start.9
  513.8 4.0 collective-permute-start.2
  684.4 7.9 collective-permute-start.3
  684.5 2.3 copy-start.20
  684.5 2.4 copy-start.22
  686.9 2.6 copy-start.16
  686.9 2.6 copy-start.18
  692.2 1.1 copy-start.12
  692.2 1.4 copy-start.14
  693.6 2.6 copy-start.3
  693.6 2.6 copy-start.24
  693.6 2.6 copy-start.26
  696.3 3.5 copy-start.6
  699.8 3.2 copy-start.8
  699.8 3.2 copy-start.10
  702.5 4.0 collective-permute-start.4
  706.6 1.2 copy-start.29
  707.7 93.6 %copy-start.31 = (s32[640]{0:T(1024)S(1)}, s32[640]{0:T(1024)}, u32[]{:S(2)}) copy-start(s32[640]{0:T(1024)} %param.21) | copy-start | bytes 7684
  801.1 0.7 copy-start.1
  801.1 5.6 collective-permute-start.5
  806.7 1.2 copy-start.28
  897.8 42.6 %all-to-all-start.4 = ((f32[8,4,40,640]{3,2,0,1:T(8,128)}), f32[8,4,40,640]{3,2,0,1:T(8,128)}, u32[]{:S(2)}, u32[]{:S(2)}) async-start(f32[8,4,40,640]{3,2,0,1:T(8,128)} %copy.57), calls=%async_computation.4 | async-start | bytes 6553600 | tf_op jit(solution)/shard_map/all_to_all | solution.py:760
  940.4 3.7 copy-start.35
  949.5 41.8 %all-to-all-start.5 = ((f32[4,8,40,640]{3,2,1,0:T(8,128)}), f32[4,8,40,640]{3,2,1,0:T(8,128)}, u32[]{:S(2)}, u32[]{:S(2)}) async-start(f32[4,8,40,640]{3,2,1,0:T(8,128)} %copy.60), calls=%async_computation.5 | async-start | bytes 6553600 | tf_op jit(solution)/shard_map/all_to_all | solution.py:772

commit v2 on v1

--- a/solution.py
+++ b/solution.py
@@ -370,15 +370,29 @@
     beyond = jnp.sqrt((following * following - square) / (4.0 * following * following - 1.0))
     lower = jnp.where(live, -(degree - 1.0) * here, 0.0)
     upper = jnp.where(ahead_live, (degree + 2.0) * beyond, 0.0)
-    ahead = jnp.sqrt(
-        (4.0 * following * following - 1.0) / (following * following - square)
-    )
-    return lower, upper, live.astype(jnp.float32), ahead, here
-
-
-def half_table_kernel(coefficient_ref, start_ref, cos_ref, high_ref, low_ref, *, size):
+    return lower, upper, live.astype(jnp.float32)
+
+
+def recurrence_factors(parity, size):
+    width, _ = packed_width(size)
+    orders = 2 * jnp.asarray(order_list(size)) + parity
+    shape = (orders.shape[0], width // 16, GROUP, 32)
+    lane = lax.broadcasted_iota(jnp.int32, shape, 3)
+    position = 16 * lax.broadcasted_iota(jnp.int32, shape, 1) + lane % 16
+    split = size - 2 * GROUP * lax.broadcasted_iota(jnp.int32, shape, 0)
+    wave = jnp.where(position < split, orders[:, None, 0, :, None], orders[:, None, 1, :, None])
+    degree = wave + jnp.where(position < split, position, position - split)
+    wave, degree = wave.astype(jnp.float32), degree.astype(jnp.float32)
+    square, following = wave * wave, degree + 1.0
+    ahead = (4.0 * following * following - 1.0) / (following * following - square)
+    behind = (degree * degree - square) / (4.0 * degree * degree - 1.0)
+    return jnp.sqrt(jnp.where(lane < 16, ahead, behind))
+
+
+def half_table_kernel(coefficient_ref, start_ref, cos_ref, *refs, size, first_pair):
+    high_ref, low_ref = refs[-2:]
     lats = cos_ref.shape[1]
-    pair = pl.program_id(0)
+    pair = pl.program_id(0) + first_pair
     spans = [(k, min(LANES, lats - k)) for k in range(0, lats, LANES)]
     mus = [jnp.broadcast_to(cos_ref[0:1, k : k + n], (GROUP, n)) for k, n in spans]
     blocks = coefficient_ref.shape[1]
@@ -434,42 +448,42 @@
     lax.fori_loop(0, blocks, block, tuple(fresh(0, k, n) for k, n in spans))
 
 
-def half_table(parity, cosines, sines, ahead, behind, size):
-    width, _ = packed_width(size)
+def table_starts(parity, sines, size):
     orders = 2 * jnp.asarray(order_list(size)) + parity
-    pairs, lats = orders.shape[0], cosines.shape[0]
     wavenum = orders.reshape(-1).astype(jnp.float32)[:, None]
     counter = jnp.arange(1, size, dtype=jnp.int32).astype(jnp.float32)
     halves = 0.5 * jnp.log((2.0 * counter + 1.0) / (2.0 * counter))
     start_log = jnp.sum(jnp.where(counter[None, :] <= wavenum, halves[None, :], 0.0), axis=1)
     log_start = -0.5 * math.log(2.0) + start_log[:, None] + wavenum * jnp.log(sines)[None, :]
-    log_start = log_start.reshape(pairs, 2, GROUP, lats)
-    blocks = width // 16
-
-    def by_block(array):
-        return jnp.swapaxes(array[:, :, :width].reshape(pairs, GROUP, blocks, 16), 1, 2)
-
-    coefficients = jnp.concatenate([by_block(ahead), by_block(behind)], axis=3)
-    table = jax.ShapeDtypeStruct((pairs, GROUP, width, lats), jnp.bfloat16)
-    table_spec = pl.BlockSpec((1, GROUP, width, lats), lambda g: (g, 0, 0, 0))
+    return log_start.reshape(orders.shape + (sines.shape[0],))
+
+
+def half_table(factors, starts, cosines, size, first_pair, count, table=()):
+    width, _ = packed_width(size)
+    pairs, blocks = factors.shape[:2]
+    lats = cosines.shape[0]
+    shape = jax.ShapeDtypeStruct((pairs, GROUP, width, lats), jnp.bfloat16)
+    table_spec = pl.BlockSpec((1, GROUP, width, lats), lambda g: (g + first_pair, 0, 0, 0))
     return pl.pallas_call(
-        functools.partial(half_table_kernel, size=size),
-        grid=(pairs,),
+        functools.partial(half_table_kernel, size=size, first_pair=first_pair),
+        grid=(count,),
         in_specs=[
-            pl.BlockSpec((1, blocks, GROUP, 32), lambda g: (g, 0, 0, 0)),
-            pl.BlockSpec((1, 2, GROUP, lats), lambda g: (g, 0, 0, 0)),
+            pl.BlockSpec((1, blocks, GROUP, 32), lambda g: (g + first_pair, 0, 0, 0)),
+            pl.BlockSpec((1, 2, GROUP, lats), lambda g: (g + first_pair, 0, 0, 0)),
             pl.BlockSpec((1, lats), lambda g: (0, 0)),
-        ],
+        ]
+        + [pl.BlockSpec(memory_space=pl.ANY)] * len(table),
         out_specs=[table_spec, table_spec],
-        out_shape=[table, table],
+        out_shape=[shape, shape],
+        input_output_aliases={3: 0, 4: 1} if table else {},
         compiler_params=pltpu.CompilerParams(vmem_limit_bytes=VMEM),
         cost_estimate=pl.CostEstimate(
-            flops=pairs * GROUP * width * lats * 10,
-            bytes_accessed=pairs * GROUP * width * lats * 4,
+            flops=count * GROUP * width * lats * 2000,
+            bytes_accessed=count * GROUP * width * lats * 4,
             transcendentals=0,
         ),
         name="half_table",
-    )(coefficients, log_start, cosines[None, :])
+    )(factors, starts, cosines[None, :], *table)
 
 
 def split_halves(value):
@@ -582,7 +596,7 @@
             )
         return carry
 
-    lax.fori_loop(0, GROUP, one_slot, 0)
+    lax.fori_loop(0, GROUP, one_slot, 0, unroll=True)
     for which, result in ((0, firsts), (1, seconds)):
         turned = jnp.swapaxes(result[...], 0, 1)
         if stage == "last":
@@ -636,7 +650,7 @@
         ],
         compiler_params=pltpu.CompilerParams(vmem_limit_bytes=VMEM),
         cost_estimate=pl.CostEstimate(
-            flops=pairs * GROUP * width * lats * 200,
+            flops=pairs * GROUP * width * lats * 2000,
             bytes_accessed=pairs * GROUP * width * lats * 4,
             transcendentals=0,
         ),
@@ -662,10 +676,14 @@
         return lax.all_to_all(array, "wave", split_axis=0, concat_axis=0, tiled=True)
 
     every = jnp.arange(size, dtype=jnp.int32)
-    slot_of = jnp.zeros((size,), jnp.int32).at[wave_order].set(every)
-    lat_slot_of = jnp.zeros((lats,), jnp.int32).at[lat_order].set(
-        jnp.arange(lats, dtype=jnp.int32)
-    )
+
+    def places(values, order):
+        spots = jnp.arange(order.shape[0], dtype=jnp.int32)[None, :]
+        return jnp.sum(jnp.where(order[None, :] == values[:, None], spots, 0), axis=1)
+
+    def take_rows(array, rows):
+        return array.at[rows].get(mode="promise_in_bounds")
+
     order = order_list(size)
     pairs = order.shape[0]
     flat_order = jnp.asarray(order.reshape(-1))
@@ -673,21 +691,26 @@
     spread = to_levels(jnp.swapaxes(vorticity, 0, 1)).reshape(devices * comps * slots, size)
 
     def rows_of(which):
-        slot = jnp.take(slot_of, 2 * flat_order + which)
+        slot = places(2 * flat_order + which, wave_order)
         row = (slot // slots) * (comps * slots) + slot % slots
-        rows = jnp.take(spread, jnp.concatenate([row, row + slots]), axis=0)
+        rows = take_rows(spread, jnp.concatenate([row, row + slots]))
         return rows.reshape(comps, pairs, 2, GROUP, size)
 
     north = jnp.arange(half_lats, dtype=jnp.int32)
     cosines, sines, weights = latitudes(north)
-    lower, upper, live, ahead, behind = packed_coupling(parity, size)
-    table = half_table(parity, cosines, sines, ahead, behind, size)
-
-    lat_rows = jnp.take(lat_slot_of, jnp.concatenate([north, lats - 1 - north]))
-
-    def wind_of(wind):
-        rows = to_levels(wind).reshape(lats, longitudes)
-        return jnp.take(rows, lat_rows, axis=0)
+    lower, upper, live = packed_coupling(parity, size)
+    factors = recurrence_factors(parity, size)
+    starts = table_starts(parity, sines, size)
+    table = half_table(factors, starts, cosines, size, 0, pairs // 2)
+    winds = jnp.concatenate([wind_lam, wind_mu], axis=1)
+    winds = winds + 0.0 * (spread[0, 0] + table[0][0, 0, 0, 0].astype(jnp.float32))
+    winds = to_levels(winds).reshape(2 * lats, longitudes)
+    table = half_table(
+        factors, starts, cosines, size, pairs // 2, pairs - pairs // 2, tuple(table)
+    )
+
+    lat_slot = places(jnp.concatenate([north, lats - 1 - north]), lat_order)
+    lat_rows = (lat_slot // lat_slots) * (2 * lat_slots) + lat_slot % lat_slots
 
     sign = 1.0 - 2.0 * parity.astype(jnp.float32)
     row_scale = jnp.concatenate([weights, weights])[:, None] / longitudes
@@ -732,7 +755,7 @@
 
     own_q, other_q = rows_of(parity), exchange(rows_of(1 - parity))
     start, own_a, other_a = visit("first", table, [lower, upper, live], [own_q, other_q], size)
-    wind_l, wind_m = wind_of(wind_lam), wind_of(wind_mu)
+    wind_l, wind_m = take_rows(winds, lat_rows), take_rows(winds, lat_rows + lat_slots)
     own_b, other_b = tendency_rows(own_a, other_a, wind_l, wind_m)
     first_rate, own_a, other_a = visit(
         "middle", table, [lower, upper, live], [own_b, other_b, start], size
@@ -744,14 +767,11 @@
     stacked = jnp.concatenate(
         [own_q.reshape(comps * size // 2, size), received.reshape(comps * size // 2, size)], axis=0
     )
-    place = jnp.zeros((size // 2,), jnp.int32).at[flat_order].set(
-        jnp.arange(size // 2, dtype=jnp.int32)
-    )
     wave_rows = wave_order.reshape(devices, 1, slots)
-    row = jnp.take(place, wave_rows // 2)
+    row = places(wave_order // 2, flat_order).reshape(devices, 1, slots)
     row = row + jnp.where(wave_rows % 2 == parity, 0, comps * size // 2)
     row = row + (size // 2) * jnp.arange(comps, dtype=jnp.int32)[None, :, None]
-    leaving = jnp.take(stacked, row.reshape(-1), axis=0).reshape(devices, comps * slots, size)
+    leaving = take_rows(stacked, row.reshape(-1)).reshape(devices, comps * slots, size)
     advanced = to_levels(leaving)
 
     lev_count = modes.shape[0] // levels

time: 1000 us -> 724 us (0.72)
  Pallas kernels: 506 us -> 402 us
  blocking collectives: 159 us -> 79.3 us
  waiting for transfers between devices: 142 us -> 74.5 us
  local copies, waits for them, and re-layouts: 89.3 us -> 55.5 us
    pallas_call x3, Pallas kernels: 343 us -> 235 us  [visit(): pl.pallas_call(functools.partial(visit_kernel, size=size, stage=stage), g...]
    all_to_all x2 -> x1, blocking collectives: 159 us -> 79.3 us  [to_levels(): lax.all_to_all(array, 'wave', split_axis=0, concat_axis=0, tiled=True)]
    all_to_all x2, waiting for transfers between devices: 70.5 us -> 0.01 us  [to_levels(): lax.all_to_all(array, 'wave', split_axis=0, concat_axis=0, tiled=True)]
    select_n x12 -> x5, other arithmetic: 11.6 us -> 0.24 us  [the longest x4 0.23 us: take_rows(): return array.at[rows].get(mode='promise_in_bounds')]
    gather x10 -> x5, local copies, waits for them, and re-layouts: 37.6 us -> 27 us  [take_rows(): return array.at[rows].get(mode='promise_in_bounds')]
    cos x2 -> x0, other arithmetic: 10.5 us -> none  [trigonometric(): cos, sin = (jnp.cos(angles), jnp.sin(angles))]
    pallas_call x1 -> x2, Pallas kernels: 163 us -> 167 us  [half_table(): pl.pallas_call(functools.partial(half_table_kernel, size=size, first_pair...]
  transfers between devices with their start and end apart: 10 -> 10, of which waited for: 3 -> 3; matrix products, arithmetic and copies ran while one was open for 11% -> 9% of each run, Pallas kernels for 25% -> 31%
where the time goes in v2:
time: 724 us; the launch traced here: 715 us
  Pallas kernels  402 us (56%)
  blocking collectives  79.3 us (11%)
  waiting for transfers between devices  74.5 us (10%)
  local copies, waits for them, and re-layouts  55.5 us (8%)
  matrix products  48 us (7%)
  other arithmetic  29.8 us (4%)
  starting transfers between devices  23 us (3%)
    pallas_call x3, Pallas kernels, visit(): pl.pallas_call(functools.partial(visit_kernel, size=size, stage=stage), g...  235 us
    pallas_call x2, Pallas kernels, half_table(): pl.pallas_call(functools.partial(half_table_kernel, size=size, first_pair...  167 us
    all_to_all x1, blocking collectives, to_levels(): lax.all_to_all(array, 'wave', split_axis=0, concat_axis=0, tiled=True)  79.3 us
    all_to_all x1, waiting for transfers between devices, by_level(): lax.all_to_all(pieces, 'lev', split_axis=1, concat_axis=0, tiled=True)  36.5 us
    all_to_all x1, waiting for transfers between devices, by_level(): lax.all_to_all(restored.reshape(lev_count, levels, rows_each, size), 'lev...  35.2 us
    gather x5, local copies, waits for them, and re-layouts, take_rows(): return array.at[rows].get(mode='promise_in_bounds')  27 us
    dot_general x4, matrix products, grid(): jnp.einsum('sr,sk->rk', theirs, table_other, precision=HIGH_ACCURACY)  17.6 us
  transfers between devices with their start and end apart: 10, of which 3 were waited for; matrix products, arithmetic and copies ran while one was open for 9% of the time, Pallas kernels for 31%

profile of v2, /device:TPU:0, one launch (start us, length us, event | category | flops | bytes accessed | tf_op | source)
XLA Modules:
  0.0 715.1 jit_solution(14143526183851513397)
XLA Ops:
  0.6 3.9 copy.68
  4.5 6.5 all-to-all-start
  11.8 0.6 multiply_cosine_fusion.cos_ref
  12.5 0.9 multiply_add_fusion.start_ref
  13.5 4.8 fusion.6.coefficient_ref
  18.3 83.4 %half_table.2 = (bf16[20,8,656,320]{3,2,1,0:T(8,128)(2,1)}, bf16[20,8,656,320]{3,2,1,0:T(8,128)(2,1)}) custom-call(f32[20,41,8,32]{3,2,1,0:T(8,128)} %fusion.6.coefficient_ref, f32[20,2,8,320]{3,2,1,0:T(8,128)} %multiply_add_fusion.start_ref, f32[1,320]{1,0:T(1,128)} %multiply_cosine_fusion.cos_ref), custom_call_target="tpu_custom_call" | custom-call | flops 33587200000 | bytes 67174400 | tf_op jit(solution)/shard_map/half_table/pallas_call | solution.py:467
  101.6 1.2 slice.63
  102.8 0.4 select_reduce_fusion.2
  103.3 0.5 slice.90
  103.9 3.3 gather_fusion.2
  107.1 0.5 collective-permute-start
  108.9 6.3 maximum_add_fusion
  115.2 4.8 all-to-all-start.1
  120.0 83.6 %half_table.3 = (bf16[20,8,656,320]{3,2,1,0:T(8,128)(2,1)}, bf16[20,8,656,320]{3,2,1,0:T(8,128)(2,1)}) custom-call(f32[20,41,8,32]{3,2,1,0:T(8,128)} %fusion.6.coefficient_ref, f32[20,2,8,320]{3,2,1,0:T(8,128)} %multiply_add_fusion.start_ref, f32[1,320]{1,0:T(1,128)} %multiply_cosine_fusion.cos_ref, ...), custom_call_target="tpu_custom_call", output_to_operand_aliasing={{0}: (3, {}), {1}: (4, {})} | custom-call | flops 33587200000 | bytes 67174400 | tf_op jit(solution)/shard_map/half_table/pallas_call | solution.py:467
  203.7 1.0 fusion.70.refs_4_.refs_2_
  204.8 2.1 fusion.64
  206.9 3.3 gather_fusion.1
  210.2 56.4 %visit_first.1 = (f32[20,8,4,768]{3,2,1,0:T(4,128)}, f32[4,20,2,8,640]{4,3,2,1,0:T(8,128)}, f32[4,20,2,8,640]{4,3,2,1,0:T(8,128)}) custom-call(bf16[20,8,656,320]{3,2,1,0:T(8,128)(2,1)} %get-tuple-element.16.refs_0_, bf16[20,8,656,320]{3,2,1,0:T(8,128)(2,1)} %get-tuple-element.17.refs_1_, f32[20,8,768]{2,1,0:T(8,128)} %get-tuple-element.55.refs_2_, ...), custom_call_target="tpu_custom_call" | custom-call | flops 67174400000 | bytes 134348800 | tf_op jit(solution)/shard_map/visit_first/pallas_call | solution.py:640
  266.6 0.4 collective-permute-start.1
  267.1 0.3 select_reduce_fusion
  267.6 4.9 fusion.44
  272.6 4.9 fusion.50
  277.5 0.3 fusion.114
  277.9 0.6 copy-done.18
  278.7 3.7 fusion.33
  282.4 3.8 fusion.29
  286.1 1.4 fusion.113
  287.5 3.7 fusion.31
  291.3 7.4 %gather_fusion = f32[640,1280]{1,0:T(8,128)S(1)} fusion(f32[1280,1280]{1,0:T(8,128)} %bitcast.6, s32[1024]{0:T(1024)S(1)} %get-tuple-element.89), kind=kCustom, calls=%fused_computation | custom fusion | bytes 6556160 | tf_op jit(solution)/shard_map/gather | solution.py:685
  298.7 8.3 %gather_fusion.3 = f32[640,1280]{1,0:T(8,128)} fusion(f32[1280,1280]{1,0:T(8,128)} %bitcast.6, s32[1024]{0:T(1024)S(1)} %get-tuple-element.88), kind=kCustom, calls=%fused_computation.3 | custom fusion | bytes 6556160 | tf_op jit(solution)/shard_map/gather | solution.py:685
  307.0 7.7 %multiply_multiply_fusion.3 = (f32[640,640]{1,0:T(8,128)S(1)}, f32[640,640]{1,0:T(8,128)S(1)}) fusion(f32[640,640]{1,0:T(8,128)} %fusion.29, f32[640,640]{1,0:T(8,128)} %fusion.33, f32[640,640]{1,0:T(8,128)} %fusion.31, f32[640,1280]{1,0:T(8,128)} %gather_fusion.3, f32[640,1280]{1,0:T(8,128)S(1)} %gather_fusion, f32[]{:T(128)S(6)} %sub.118, ...), kind=kOutput, calls=%fused_computation.50 | convolution fusion | flops 1580236800 | bytes 18024964 | tf_op jit(solution)/shard_map/sr,sk->rk/dot_general | solution.py:739
  314.7 2.5 fusion.22
  317.3 3.6 fusion.24
  320.9 1.2 copy-done.33
  322.1 114.2 %visit_middle.1 = (f32[20,8,4,768]{3,2,1,0:T(4,128)}, f32[4,20,2,8,640]{4,3,2,1,0:T(8,128)}, f32[4,20,2,8,640]{4,3,2,1,0:T(8,128)}) custom-call(bf16[20,8,656,320]{3,2,1,0:T(8,128)(2,1)} %get-tuple-element.16.refs_0_, bf16[20,8,656,320]{3,2,1,0:T(8,128)(2,1)} %get-tuple-element.17.refs_1_, f32[20,8,768]{2,1,0:T(8,128)} %get-tuple-element.55.refs_2_, ...), custom_call_target="tpu_custom_call" | custom-call | flops 67174400000 | bytes 134348800 | tf_op jit(solution)/shard_map/visit_middle/pallas_call | solution.py:640
  436.2 0.5 collective-permute-start.3
  436.7 2.3 fusion.112
  439.1 2.6 fusion.32
  441.8 2.6 fusion.28
  444.7 0.8 copy-done.11
  445.8 2.6 fusion.30
  448.5 3.5 multiply_multiply_fusion.2
  452.1 2.7 fusion.18
  455.0 3.6 fusion.20
  458.5 1.2 copy-done.32
  459.7 64.4 %visit_last.1 = (f32[2,20,2,8,640]{4,3,2,1,0:T(8,128)}, f32[2,20,2,8,640]{4,3,2,1,0:T(8,128)}) custom-call(bf16[20,8,656,320]{3,2,1,0:T(8,128)(2,1)} %get-tuple-element.16.refs_0_, bf16[20,8,656,320]{3,2,1,0:T(8,128)(2,1)} %get-tuple-element.17.refs_1_, f32[20,8,768]{2,1,0:T(8,128)} %fusion.70.refs_4_.refs_2_, f32[2,20,2,8,640]{4,3,2,1,0:T(8,128)} %bitcast.86, ...), custom_call_target="tpu_custom_call" | custom-call | flops 67174400000 | bytes 134348800 | tf_op jit(solution)/shard_map/visit_last/pallas_call | solution.py:640
  524.1 0.4 collective-permute-start.5
  525.0 2.8 collective-permute-done.5
  527.8 1.2 copy-done.25
  529.0 2.1 pad_maximum_fusion
  531.1 4.8 gather_fusion.4
  535.9 79.3 %all_to_all.35 = f32[8,160,640]{2,1,0:T(8,128)S(1)} all-to-all(f32[8,160,640]{2,1,0:T(8,128)} %bitcast.75), channel_id=1, replica_groups=mesh['lev'=4,'wave'=8] {'wave'}, dimensions={0} | all-to-all | bytes 6553600 | tf_op jit(solution)/shard_map/all_to_all | solution.py:676
  615.2 1.9 copy.56
  617.1 4.9 all-to-all-start.3
  622.1 0.8 gather_fusion.5
  623.1 36.5 %all-to-all-done.3 = f32[8,4,40,640]{3,2,0,1:T(8,128)} async-done(((f32[8,4,40,640]{3,2,0,1:T(8,128)}), f32[8,4,40,640]{3,2,0,1:T(8,128)}, u32[]{:S(2)}, u32[]{:S(2)}) %all-to-all-start.3) | async-done | bytes 3276832 | tf_op jit(solution)/shard_map/all_to_all | solution.py:780
  659.7 3.7 fusion.13
  663.4 1.7 multiply_bitcast_fusion
  665.1 3.6 copy.59
  668.7 4.7 all-to-all-start.4
  673.4 1.9 copy.61
  675.3 35.2 %all-to-all-done.4 = f32[4,8,40,640]{3,2,1,0:T(8,128)} async-done(((f32[4,8,40,640]{3,2,1,0:T(8,128)}), f32[4,8,40,640]{3,2,1,0:T(8,128)}, u32[]{:S(2)}, u32[]{:S(2)}) %all-to-all-start.4) | async-done | bytes 3276832 | tf_op jit(solution)/shard_map/all_to_all | solution.py:792
  710.5 2.2 copy.60
  712.7 1.9 copy.62
  (128 shorter events, 3.3 us)
Async XLA Ops:
  0.6 659.0 %copy-start = (f32[32,32]{1,0:T(8,128)S(1)}, f32[32,32]{1,0:T(8,128)}, u32[]{:S(2)}) copy-start(f32[32,32]{1,0:T(8,128)} %param.14) | copy-start | bytes 12292
  4.5 6.5 copy-start.28
  4.5 98.8 %all-to-all-start = ((f32[8,2,80,640]{3,2,1,0:T(8,128)}), f32[8,2,80,640]{3,2,1,0:T(8,128)S(1)}, u32[]{:S(2)}, u32[]{:S(2)}) async-start(f32[8,2,80,640]{3,2,1,0:T(8,128)} %bitcast.73), calls=%async_computation | async-start | bytes 6553600 | tf_op jit(solution)/shard_map/all_to_all | solution.py:676
  18.3 84.5 %copy-start.29 = (s32[320]{0:T(512)S(1)}, s32[320]{0:T(512)}, u32[]{:S(2)}) copy-start(s32[320]{0:T(512)} %constant.203) | copy-start | bytes 3844
  18.3 84.5 %copy-start.26 = (s32[640]{0:T(1024)S(1)}, s32[640]{0:T(1024)}, u32[]{:S(2)}) copy-start(s32[640]{0:T(1024)} %param.16) | copy-start | bytes 7684
  107.1 103.0 %collective-permute-start = (f32[2,20,2,8,640]{4,3,2,1,0:T(8,128)}, f32[2,20,2,8,640]{4,3,2,1,0:T(8,128)}, u32[]{:S(2)}, u32[]{:S(2)}) collective-permute-start(f32[2,20,2,8,640]{4,3,2,1,0:T(8,128)} %bitcast.90), channel_id=1, source_target_pairs={{0,1},{1,0},{2,3},{3,2},{4,5},{5,4},{6,7},{7,6},{8,9},{9,8},{10,11... | collective-permute-start | bytes 4915208 | tf_op jit(solution)/shard_map/ppermute | solution.py:673
  115.2 176.1 %all-to-all-start.1 = ((f32[8,160,1280]{2,1,0:T(8,128)}), f32[8,160,1280]{2,1,0:T(8,128)}, u32[]{:S(2)}, u32[]{:S(2)}) async-start(f32[8,160,1280]{2,1,0:T(8,128)} %maximum_add_fusion), calls=%async_computation.1 | async-start | bytes 13107200 | tf_op jit(solution)/shard_map/all_to_all | solution.py:676
  210.1 56.9 %copy-start.30 = (s32[640]{0:T(1024)S(1)}, s32[640]{0:T(1024)}, u32[]{:S(2)}) copy-start(s32[640]{0:T(1024)} %param.17) | copy-start | bytes 7684
  266.6 19.6 %collective-permute-start.1 = (f32[4,20,2,8,640]{4,3,2,1,0:T(8,128)}, f32[4,20,2,8,640]{4,3,2,1,0:T(8,128)S(1)}, u32[]{:S(2)}, u32[]{:S(2)}) collective-permute-start(f32[4,20,2,8,640]{4,3,2,1,0:T(8,128)} %get-tuple-element.19), channel_id=1, source_target_pairs={{0,1},{1,0},{2,3},{3,2},{4,5},{5,4},{6,7},{7,6},{8,9},{9,8},{10,11... | collective-permute-start | bytes 9830408 | tf_op jit(solution)/shard_map/ppermute | solution.py:673
  272.6 15.0 %copy-start.10 = (f32[320,640]{1,0:T(8,128)}, f32[320,640]{1,0:T(8,128)S(1)}, u32[]{:S(2)}) copy-start(f32[320,640]{1,0:T(8,128)S(1)} %get-tuple-element.62) | copy-start | bytes 2457604
  272.6 15.0 %copy-start.12 = (f32[320,640]{1,0:T(8,128)}, f32[320,640]{1,0:T(8,128)S(1)}, u32[]{:S(2)}) copy-start(f32[320,640]{1,0:T(8,128)S(1)} %get-tuple-element.63) | copy-start | bytes 2457604
  272.6 5.0 copy-start.24
  277.5 1.0 copy-start.18
  277.5 1.2 copy-start.20
  277.5 4.9 copy-start.14
  277.5 4.9 copy-start.16
  307.0 7.7 %copy-start.2 = (f32[320,640]{1,0:T(8,128)S(1)}, f32[320,640]{1,0:T(8,128)}, u32[]{:S(2)}) copy-start(f32[320,640]{1,0:T(8,128)} %get-tuple-element.66) | copy-start | bytes 2457604
  307.0 7.7 %copy-start.4 = (f32[320,640]{1,0:T(8,128)S(1)}, f32[320,640]{1,0:T(8,128)}, u32[]{:S(2)}) copy-start(f32[320,640]{1,0:T(8,128)} %get-tuple-element.67) | copy-start | bytes 2457604
  314.7 2.6 copy-start.6
  314.7 2.6 copy-start.8
  317.2 3.7 collective-permute-start.2
  320.9 1.2 copy-start.33
  436.2 8.2 %collective-permute-start.3 = (f32[4,20,2,8,640]{4,3,2,1,0:T(8,128)}, f32[4,20,2,8,640]{4,3,2,1,0:T(8,128)S(1)}, u32[]{:S(2)}, u32[]{:S(2)}) collective-permute-start(f32[4,20,2,8,640]{4,3,2,1,0:T(8,128)} %get-tuple-element.22), channel_id=1, source_target_pairs={{0,1},{1,0},{2,3},{3,2},{4,5},{5,4},{6,7},{7,6},{8,9},{9,8},{10,11... | collective-permute-start | bytes 9830408 | tf_op jit(solution)/shard_map/ppermute | solution.py:673
  436.7 2.4 copy-start.19
  436.7 2.4 copy-start.21
  439.1 2.7 copy-start.15
  439.1 2.7 copy-start.17
  444.4 1.1 copy-start.11
  444.4 1.4 copy-start.13
  445.8 2.6 copy-start.1
  445.8 2.7 copy-start.22
  445.8 2.7 copy-start.23
  448.5 3.6 copy-start.3
  448.5 3.6 copy-start.5
  452.1 2.9 copy-start.7
  452.1 2.9 copy-start.9
  454.8 3.7 collective-permute-start.4
  458.5 1.2 copy-start.32
  459.7 64.8 %copy-start.27 = (s32[640]{0:T(1024)S(1)}, s32[640]{0:T(1024)}, u32[]{:S(2)}) copy-start(s32[640]{0:T(1024)} %param.16) | copy-start | bytes 7684
  459.7 64.9 %copy-start.31 = (s32[320]{0:T(512)S(1)}, s32[320]{0:T(512)}, u32[]{:S(2)}) copy-start(s32[320]{0:T(512)} %constant.200.clone) | copy-start | bytes 3844
  524.1 3.8 collective-permute-start.5
  527.8 1.2 copy-start.25
  617.1 42.6 %all-to-all-start.3 = ((f32[8,4,40,640]{3,2,0,1:T(8,128)}), f32[8,4,40,640]{3,2,0,1:T(8,128)}, u32[]{:S(2)}, u32[]{:S(2)}) async-start(f32[8,4,40,640]{3,2,0,1:T(8,128)} %copy.56), calls=%async_computation.3 | async-start | bytes 6553600 | tf_op jit(solution)/shard_map/all_to_all | solution.py:780
  659.7 3.7 copy-start.34
  668.7 41.8 %all-to-all-start.4 = ((f32[4,8,40,640]{3,2,1,0:T(8,128)}), f32[4,8,40,640]{3,2,1,0:T(8,128)}, u32[]{:S(2)}, u32[]{:S(2)}) async-start(f32[4,8,40,640]{3,2,1,0:T(8,128)} %copy.59), calls=%async_computation.4 | async-start | bytes 6553600 | tf_op jit(solution)/shard_map/all_to_all | solution.py:792
